TPU v7x, 256 devices: a whole 4x4x8 slice. The times are simulated.
256 devices in a mesh: along: 32 (over z, x), cross: 2 (over core), batch: 4 (over y).
Axes of the slice: x: 4, y: 4, z: 8, core: 2. Of those that a mesh axis runs over, the one named last changes fastest.
Arguments:
- pressure_start: float32 [4, 16, 2048, 256], P('batch', None, 'along', 'cross'), may hold values from -6 to 6
- along_start: float32 [4, 16, 2048, 256], P('batch', None, 'along', 'cross'), may hold values from -6 to 6
- cross_start: float32 [4, 16, 2048, 256], P('batch', None, 'along', 'cross'), may hold values from -6 to 6
- depth_layers: int32 [2048, 256], P('along', 'cross'), may hold values from 1 to 16
- stiffness: float32 [2048, 256], P('along', 'cross'), may hold values from 0.1 to 0.45
- patch_lists: int32 [4, 4096], P('batch'), may hold values from 0 to 8191, all different within a row
- owner_map: int32 [64, 128], P(('along', 'cross')), may hold values from 0 to 63, as said below
Outputs:
- adjoint_pressure: float32 [4, 16, 2048, 256], P('batch', None, 'along', 'cross')
- panel_store: float32 [64, 192, 4, 512], P(('along', 'cross'), None, 'batch')
Inputs may be any that keep to these rules, and one draw needn't show every extreme that they name: `owner_map`: each entry is an owner, numbered as the grid blocks. Of the 128 patches of one block at most 3 have one owner, and in every draw some owner holds exactly 3 patches of every block. `patch_lists`: each row names 4096 different patch ids; every patch is named by some row.
All inputs are finite; a program needn't handle non-finite values.
Results may differ from a plain program's by a relative error of at most 0.0003.
Values sent between devices are 32-bit elements; how exact they have to be, the bound alone decides.
A program may use at most 64 MiB of HBM per device.

v0:
```python
import jax
import jax.numpy as jnp
from jax import lax
from jax.sharding import PartitionSpec as P

STEPS = 8


def from_behind(shard, axis, by):
    size = lax.axis_size(axis)
    pairs = [(i, i + by) for i in range(size) if 0 <= i + by < size]
    return lax.ppermute(shard, axis, pairs)


def column_masks(depth, layers):
    row_count, col_count = depth.shape
    layer_index = lax.broadcasted_iota(jnp.int32, (layers, row_count, col_count), 0)
    wet_mask = (layer_index < depth[None]).astype(jnp.float32)
    onehot = (layer_index == depth[None] - 1).astype(jnp.float32)
    zero_layer = jnp.zeros((1, row_count, col_count), jnp.float32)
    wet_upper = jnp.concatenate([zero_layer, wet_mask[:-1]], 0)
    wet_lower = jnp.concatenate([wet_mask[1:], zero_layer], 0)
    return (wet_mask, onehot, wet_upper, wet_lower)


def run_steps(pressure, flow_along, flow_cross, depth, stiffness, edges_ahead, edges_behind):
    sensors, layers, row_count, col_count = pressure.shape
    wet_mask, onehot, wet_upper, wet_lower = column_masks(depth, layers)
    zero_sensor_layer = jnp.zeros((sensors, 1, row_count, col_count), jnp.float32)
    traces = []
    for step_index in range(STEPS):
        ahead_row, ahead_col = edges_ahead(pressure)
        flow_along = wet_mask * (
            flow_along - (jnp.concatenate([pressure[:, :, 1:, :], ahead_row], 2) - pressure)
        )
        flow_cross = wet_mask * (
            flow_cross - (jnp.concatenate([pressure[:, :, :, 1:], ahead_col], 3) - pressure)
        )
        behind_row, behind_col = edges_behind(flow_along, flow_cross)
        behind = jnp.concatenate([behind_row, flow_along[:, :, :-1, :]], 2)
        before = jnp.concatenate([behind_col, flow_cross[:, :, :, :-1]], 3)
        upper_layer = jnp.concatenate([zero_sensor_layer, pressure[:, :-1]], 1)
        lower_layer = jnp.concatenate([pressure[:, 1:], zero_sensor_layer], 1)
        vertical = wet_upper * (upper_layer - pressure) + wet_lower * (lower_layer - pressure)
        pressure = wet_mask * (
            pressure
            - stiffness * (flow_along - behind + (flow_cross - before))
            + 0.5 * stiffness * vertical
        )
        traces.append(jnp.sum(pressure * onehot, axis=1))
    return (pressure, jnp.stack(traces, 1))


def shards(
    pressure_start, along_start, cross_start, depth_layers, stiffness, patch_lists, owner_map
):
    sensors, layers, row_count, col_count = pressure_start.shape

    def shift_ahead(pressure):
        ahead_row = from_behind(pressure[:, :, 0:1, :], "along", -1)
        ahead_col = from_behind(pressure[:, :, :, 0:1], "cross", -1)
        return (ahead_row, ahead_col)

    def shift_behind(flow_along, flow_cross):
        behind_row = from_behind(flow_along[:, :, -1:, :], "along", 1)
        behind_col = from_behind(flow_cross[:, :, :, -1:], "cross", 1)
        return (behind_row, behind_col)

    pressure, trace_all = run_steps(
        pressure_start, along_start, cross_start, depth_layers, stiffness, shift_ahead, shift_behind
    )
    patch_count = 2 * row_count
    patch_width = col_count // 2
    owner_count = lax.axis_size("along") * lax.axis_size("cross")
    capacity = patch_count // owner_count + 1
    slot_count = owner_count * capacity
    first_patch = (
        lax.axis_index("along") * lax.axis_size("cross") + lax.axis_index("cross")
    ) * patch_count
    local_ids = patch_lists - first_patch
    positions = jnp.arange(patch_count, dtype=jnp.int32)
    member = jnp.any(local_ids[:, :, None] == positions[None, None, :], axis=1).astype(jnp.float32)
    panels = trace_all.reshape(sensors, STEPS, patch_count, patch_width) * member[:, None, :, None]
    owners = owner_map[0]
    earlier = positions[None, :] < positions[:, None]
    slot_rank = jnp.sum(((owners[:, None] == owners[None, :]) & earlier).astype(jnp.int32), axis=1)
    target = owners * capacity + slot_rank
    placement = (jnp.arange(slot_count, dtype=jnp.int32)[:, None] == target[None, :]).astype(
        jnp.float32
    )
    outgoing = jnp.einsum("nj,stjc->nstc", placement, panels, precision=lax.Precision.HIGHEST)
    outgoing = outgoing.reshape(slot_count, sensors, STEPS * patch_width)
    received = lax.all_to_all(outgoing, ("along", "cross"), split_axis=0, concat_axis=0, tiled=True)
    return (pressure, received[None])


def solution(mesh):
    in_specs = (
        P("batch", None, "along", "cross"),
        P("batch", None, "along", "cross"),
        P("batch", None, "along", "cross"),
        P("along", "cross"),
        P("along", "cross"),
        P("batch", None),
        P(("along", "cross"), None),
    )
    out_specs = (P("batch", None, "along", "cross"), P(("along", "cross"), None, "batch", None))
    return jax.shard_map(shards, mesh=mesh, in_specs=in_specs, out_specs=out_specs, check_vma=False)
```

profile of v0, /device:TPU:1, one launch (start us, length us, event | category | flops | bytes accessed | tf_op | source)
XLA Modules:
  0.0 184.8 jit_solution(5000382588730505231)
XLA Ops:
  0.6 5.1 %collective-permute-start.2 = (f32[1,16,64,1]{3,2,1,0:T(8,128)}, f32[1,16,64,1]{3,2,1,0:T(8,128)S(1)}, u32[]{:S(2)}, u32[]{:S(2)}) collective-permute-start(f32[1,16,64,1]{3,2,1,0:T(8,128)} %bitcast.130), channel_id=1, source_target_pairs={{4,0},{5,1},{6,2},{7,3},{12,8},{13,9},{14,10},{15,11},{20,16},{21,... | collective-permute-start | bytes 12296 | tf_op jit(solution)/shard_map/ppermute | solution.py:12
  5.8 0.8 slice.247
  6.6 1.4 collective-permute-start
  8.0 1.2 fusion.102
  9.5 0.9 copy-done
  12.2 1.3 collective-permute-start.3
  13.5 4.0 %collective-permute-start.1 = (f32[1,16,1,128]{3,2,1,0:T(1,128)S(1)}, f32[1,16,1,128]{3,2,1,0:T(1,128)S(1)}, u32[]{:S(2)}, u32[]{:S(2)}) collective-permute-start(f32[1,16,1,128]{3,2,1,0:T(1,128)S(1)} %slice.328), channel_id=1, source_target_pairs={{0,8},{8,16},{16,24},{24,32},{32,40},{40,48},{48,56},{56,64},{64,7... | collective-permute-start | bytes 24584 | tf_op jit(solution)/shard_map/ppermute | solution.py:12
  17.6 0.7 collective-permute-done.1
  19.0 1.3 collective-permute-start.4
  20.3 3.9 %collective-permute-start.6 = (f32[1,16,64,1]{3,2,1,0:T(8,128)S(1)}, f32[1,16,64,1]{3,2,1,0:T(8,128)S(1)}, u32[]{:S(2)}, u32[]{:S(2)}) collective-permute-start(f32[1,16,64,1]{3,2,1,0:T(8,128)S(1)} %bitcast.123), channel_id=1, source_target_pairs={{4,0},{5,1},{6,2},{7,3},{12,8},{13,9},{14,10},{15,11},{20,16},{21,... | collective-permute-start | bytes 12296 | tf_op jit(solution)/shard_map/ppermute | solution.py:12
  24.5 1.2 collective-permute-done.6
  26.3 1.3 collective-permute-start.7
  27.6 4.5 %collective-permute-start.5 = (f32[1,16,1,128]{3,2,1,0:T(1,128)S(1)}, f32[1,16,1,128]{3,2,1,0:T(1,128)S(1)}, u32[]{:S(2)}, u32[]{:S(2)}) collective-permute-start(f32[1,16,1,128]{3,2,1,0:T(1,128)S(1)} %slice.336), channel_id=1, source_target_pairs={{0,8},{8,16},{16,24},{24,32},{32,40},{40,48},{48,56},{56,64},{64,7... | collective-permute-start | bytes 24584 | tf_op jit(solution)/shard_map/ppermute | solution.py:12
  33.5 1.3 collective-permute-start.8
  34.8 4.7 %collective-permute-start.10 = (f32[1,16,64,1]{3,2,1,0:T(8,128)S(1)}, f32[1,16,64,1]{3,2,1,0:T(8,128)}, u32[]{:S(2)}, u32[]{:S(2)}) collective-permute-start(f32[1,16,64,1]{3,2,1,0:T(8,128)S(1)} %bitcast.124), channel_id=1, source_target_pairs={{4,0},{5,1},{6,2},{7,3},{12,8},{13,9},{14,10},{15,11},{20,16},{21,... | collective-permute-start | bytes 12296 | tf_op jit(solution)/shard_map/ppermute | solution.py:12
  40.4 1.4 fusion.27
  42.0 1.3 collective-permute-start.11
  43.3 4.5 %collective-permute-start.9 = (f32[1,16,1,128]{3,2,1,0:T(1,128)S(1)}, f32[1,16,1,128]{3,2,1,0:T(1,128)S(1)}, u32[]{:S(2)}, u32[]{:S(2)}) collective-permute-start(f32[1,16,1,128]{3,2,1,0:T(1,128)S(1)} %slice.346), channel_id=1, source_target_pairs={{0,8},{8,16},{16,24},{24,32},{32,40},{40,48},{48,56},{56,64},{64,7... | collective-permute-start | bytes 24584 | tf_op jit(solution)/shard_map/ppermute | solution.py:12
  48.0 0.7 collective-permute-done.9
  49.3 3.9 %collective-permute-start.14 = (f32[1,16,64,1]{3,2,1,0:T(8,128)S(1)}, f32[1,16,64,1]{3,2,1,0:T(8,128)S(1)}, u32[]{:S(2)}, u32[]{:S(2)}) collective-permute-start(f32[1,16,64,1]{3,2,1,0:T(8,128)S(1)} %bitcast.125), channel_id=1, source_target_pairs={{4,0},{5,1},{6,2},{7,3},{12,8},{13,9},{14,10},{15,11},{20,16},{21,... | collective-permute-start | bytes 12296 | tf_op jit(solution)/shard_map/ppermute | solution.py:12
  53.3 1.3 collective-permute-start.12
  54.9 3.3 %collective-permute-done.12 = f32[1,16,1,128]{3,2,1,0:T(1,128)S(1)} collective-permute-done((f32[1,16,1,128]{3,2,1,0:T(1,128)S(1)}, f32[1,16,1,128]{3,2,1,0:T(1,128)S(1)}, u32[]{:S(2)}, u32[]{:S(2)}) %collective-permute-start.12) | collective-permute-done | bytes 8224 | tf_op jit(solution)/shard_map/ppermute | solution.py:12
  58.8 1.3 collective-permute-start.15
  60.1 5.1 %collective-permute-start.13 = (f32[1,16,1,128]{3,2,1,0:T(1,128)S(1)}, f32[1,16,1,128]{3,2,1,0:T(1,128)S(1)}, u32[]{:S(2)}, u32[]{:S(2)}) collective-permute-start(f32[1,16,1,128]{3,2,1,0:T(1,128)S(1)} %slice.356), channel_id=1, source_target_pairs={{0,8},{8,16},{16,24},{24,32},{32,40},{40,48},{48,56},{56,64},{64,7... | collective-permute-start | bytes 24584 | tf_op jit(solution)/shard_map/ppermute | solution.py:12
  66.6 3.9 %collective-permute-start.18 = (f32[1,16,64,1]{3,2,1,0:T(8,128)S(1)}, f32[1,16,64,1]{3,2,1,0:T(8,128)S(1)}, u32[]{:S(2)}, u32[]{:S(2)}) collective-permute-start(f32[1,16,64,1]{3,2,1,0:T(8,128)S(1)} %bitcast.126), channel_id=1, source_target_pairs={{4,0},{5,1},{6,2},{7,3},{12,8},{13,9},{14,10},{15,11},{20,16},{21,... | collective-permute-start | bytes 12296 | tf_op jit(solution)/shard_map/ppermute | solution.py:12
  70.5 1.3 collective-permute-start.16
  72.1 4.2 %collective-permute-done.16 = f32[1,16,1,128]{3,2,1,0:T(1,128)S(1)} collective-permute-done((f32[1,16,1,128]{3,2,1,0:T(1,128)S(1)}, f32[1,16,1,128]{3,2,1,0:T(1,128)S(1)}, u32[]{:S(2)}, u32[]{:S(2)}) %collective-permute-start.16) | collective-permute-done | bytes 8224 | tf_op jit(solution)/shard_map/ppermute | solution.py:12
  76.8 1.3 collective-permute-start.19
  78.1 6.0 %collective-permute-start.17 = (f32[1,16,1,128]{3,2,1,0:T(1,128)S(1)}, f32[1,16,1,128]{3,2,1,0:T(1,128)S(1)}, u32[]{:S(2)}, u32[]{:S(2)}) collective-permute-start(f32[1,16,1,128]{3,2,1,0:T(1,128)S(1)} %slice.366), channel_id=1, source_target_pairs={{0,8},{8,16},{16,24},{24,32},{32,40},{40,48},{48,56},{56,64},{64,7... | collective-permute-start | bytes 24584 | tf_op jit(solution)/shard_map/ppermute | solution.py:12
  85.6 3.9 %collective-permute-start.22 = (f32[1,16,64,1]{3,2,1,0:T(8,128)S(1)}, f32[1,16,64,1]{3,2,1,0:T(8,128)S(1)}, u32[]{:S(2)}, u32[]{:S(2)}) collective-permute-start(f32[1,16,64,1]{3,2,1,0:T(8,128)S(1)} %bitcast.127), channel_id=1, source_target_pairs={{4,0},{5,1},{6,2},{7,3},{12,8},{13,9},{14,10},{15,11},{20,16},{21,... | collective-permute-start | bytes 12296 | tf_op jit(solution)/shard_map/ppermute | solution.py:12
  89.5 1.3 collective-permute-start.20
  91.3 3.2 %collective-permute-done.20 = f32[1,16,1,128]{3,2,1,0:T(1,128)S(1)} collective-permute-done((f32[1,16,1,128]{3,2,1,0:T(1,128)S(1)}, f32[1,16,1,128]{3,2,1,0:T(1,128)S(1)}, u32[]{:S(2)}, u32[]{:S(2)}) %collective-permute-start.20) | collective-permute-done | bytes 8224 | tf_op jit(solution)/shard_map/ppermute | solution.py:12
  95.0 1.3 collective-permute-start.23
  96.4 5.6 %collective-permute-start.21 = (f32[1,16,1,128]{3,2,1,0:T(1,128)S(1)}, f32[1,16,1,128]{3,2,1,0:T(1,128)S(1)}, u32[]{:S(2)}, u32[]{:S(2)}) collective-permute-start(f32[1,16,1,128]{3,2,1,0:T(1,128)S(1)} %slice.376), channel_id=1, source_target_pairs={{0,8},{8,16},{16,24},{24,32},{32,40},{40,48},{48,56},{56,64},{64,7... | collective-permute-start | bytes 24584 | tf_op jit(solution)/shard_map/ppermute | solution.py:12
  103.4 3.9 %collective-permute-start.26 = (f32[1,16,64,1]{3,2,1,0:T(8,128)S(1)}, f32[1,16,64,1]{3,2,1,0:T(8,128)S(1)}, u32[]{:S(2)}, u32[]{:S(2)}) collective-permute-start(f32[1,16,64,1]{3,2,1,0:T(8,128)S(1)} %bitcast.128), channel_id=1, source_target_pairs={{4,0},{5,1},{6,2},{7,3},{12,8},{13,9},{14,10},{15,11},{20,16},{21,... | collective-permute-start | bytes 12296 | tf_op jit(solution)/shard_map/ppermute | solution.py:12
  107.3 1.3 collective-permute-start.24
  108.9 3.4 %collective-permute-done.24 = f32[1,16,1,128]{3,2,1,0:T(1,128)S(1)} collective-permute-done((f32[1,16,1,128]{3,2,1,0:T(1,128)S(1)}, f32[1,16,1,128]{3,2,1,0:T(1,128)S(1)}, u32[]{:S(2)}, u32[]{:S(2)}) %collective-permute-start.24) | collective-permute-done | bytes 8224 | tf_op jit(solution)/shard_map/ppermute | solution.py:12
  112.8 1.5 collective-permute-start.27
  114.3 5.6 %collective-permute-start.25 = (f32[1,16,1,128]{3,2,1,0:T(1,128)S(1)}, f32[1,16,1,128]{3,2,1,0:T(1,128)S(1)}, u32[]{:S(2)}, u32[]{:S(2)}) collective-permute-start(f32[1,16,1,128]{3,2,1,0:T(1,128)S(1)} %slice.386), channel_id=1, source_target_pairs={{0,8},{8,16},{16,24},{24,32},{32,40},{40,48},{48,56},{56,64},{64,7... | collective-permute-start | bytes 24584 | tf_op jit(solution)/shard_map/ppermute | solution.py:12
  121.3 3.9 %collective-permute-start.30 = (f32[1,16,64,1]{3,2,1,0:T(8,128)S(1)}, f32[1,16,64,1]{3,2,1,0:T(8,128)S(1)}, u32[]{:S(2)}, u32[]{:S(2)}) collective-permute-start(f32[1,16,64,1]{3,2,1,0:T(8,128)S(1)} %bitcast.129), channel_id=1, source_target_pairs={{4,0},{5,1},{6,2},{7,3},{12,8},{13,9},{14,10},{15,11},{20,16},{21,... | collective-permute-start | bytes 12296 | tf_op jit(solution)/shard_map/ppermute | solution.py:12
  125.3 1.3 collective-permute-start.28
  126.6 1.9 %fusion = pred[128]{0:T(512)(128)(4,1)S(1)} fusion(s32[4096]{0:T(1024)S(1)} %bitcast.149), kind=kLoop, calls=%fused_computation.1 | loop fusion | flops 1048448 | bytes 16512 | tf_op jit(solution)/shard_map/reduce_or | solution.py:82
  128.7 1.5 collective-permute-done.28
  130.8 1.3 collective-permute-start.31
  132.1 5.6 %collective-permute-start.29 = (f32[1,16,1,128]{3,2,1,0:T(1,128)S(1)}, f32[1,16,1,128]{3,2,1,0:T(1,128)S(1)}, u32[]{:S(2)}, u32[]{:S(2)}) collective-permute-start(f32[1,16,1,128]{3,2,1,0:T(1,128)S(1)} %slice.396), channel_id=1, source_target_pairs={{0,8},{8,16},{16,24},{24,32},{32,40},{40,48},{48,56},{56,64},{64,7... | collective-permute-start | bytes 24584 | tf_op jit(solution)/shard_map/ppermute | solution.py:12
  138.4 1.7 select_reduce_fusion
  141.9 42.1 %all_to_all.5 = f32[192,1,512]{2,1,0:T(1,128)S(1)} all-to-all(f32[192,1,512]{2,1,0:T(1,128)S(1)} %copy.15), channel_id=1, replica_groups=mesh['along'=32,'cross'=2,'batch'=4] {'along','cross'}, dimensions={0} | all-to-all | bytes 786432 | tf_op jit(solution)/shard_map/all_to_all | solution.py:93
  184.1 0.7 copy.24
  (125 shorter events, 18.9 us)
Async XLA Ops:
  0.6 10.1 %collective-permute-start.2 = (f32[1,16,64,1]{3,2,1,0:T(8,128)}, f32[1,16,64,1]{3,2,1,0:T(8,128)S(1)}, u32[]{:S(2)}, u32[]{:S(2)}) collective-permute-start(f32[1,16,64,1]{3,2,1,0:T(8,128)} %bitcast.130), channel_id=1, source_target_pairs={{4,0},{5,1},{6,2},{7,3},{12,8},{13,9},{14,10},{15,11},{20,16},{21,... | collective-permute-start | bytes 12296 | tf_op jit(solution)/shard_map/ppermute | solution.py:12
  6.6 2.7 %copy-start.1 = (s32[64,128]{1,0:T(8,128)S(1)}, s32[64,128]{1,0:T(8,128)}, u32[]{:S(2)}) copy-start(s32[64,128]{1,0:T(8,128)} %param.10) | copy-start | bytes 98308
  6.6 4.6 %collective-permute-start = (f32[1,16,1,128]{3,2,1,0:T(1,128)S(1)}, f32[1,16,1,128]{3,2,1,0:T(1,128)S(1)}, u32[]{:S(2)}, u32[]{:S(2)}) collective-permute-start(f32[1,16,1,128]{3,2,1,0:T(1,128)S(1)} %slice.247), channel_id=1, source_target_pairs={{8,0},{16,8},{24,16},{32,24},{40,32},{48,40},{56,48},{64,56},{72,6... | collective-permute-start | bytes 24584 | tf_op jit(solution)/shard_map/ppermute | solution.py:12
  9.4 1.0 copy-start
  10.5 1.0 copy-start.3
  10.5 1.2 copy-start.4
  12.0 5.5 %copy-start.2 = (f32[64,128]{1,0:T(8,128)S(1)}, f32[64,128]{1,0:T(8,128)}, u32[]{:S(2)}) copy-start(f32[64,128]{1,0:T(8,128)} %param.11) | copy-start | bytes 98308
  12.2 5.3 %collective-permute-start.3 = (f32[1,16,64,1]{3,2,1,0:T(8,128)S(1)}, f32[1,16,64,1]{3,2,1,0:T(8,128)S(1)}, u32[]{:S(2)}, u32[]{:S(2)}) collective-permute-start(f32[1,16,64,1]{3,2,1,0:T(8,128)S(1)} %slice.330), channel_id=1, source_target_pairs={{0,4},{1,5},{2,6},{3,7},{8,12},{9,13},{10,14},{11,15},{16,20},{17,... | collective-permute-start | bytes 12296 | tf_op jit(solution)/shard_map/ppermute | solution.py:12
  13.5 4.8 %collective-permute-start.1 = (f32[1,16,1,128]{3,2,1,0:T(1,128)S(1)}, f32[1,16,1,128]{3,2,1,0:T(1,128)S(1)}, u32[]{:S(2)}, u32[]{:S(2)}) collective-permute-start(f32[1,16,1,128]{3,2,1,0:T(1,128)S(1)} %slice.328), channel_id=1, source_target_pairs={{0,8},{8,16},{16,24},{24,32},{32,40},{40,48},{48,56},{56,64},{64,7... | collective-permute-start | bytes 24584 | tf_op jit(solution)/shard_map/ppermute | solution.py:12
  19.0 6.7 %collective-permute-start.4 = (f32[1,16,1,128]{3,2,1,0:T(1,128)S(1)}, f32[1,16,1,128]{3,2,1,0:T(1,128)S(1)}, u32[]{:S(2)}, u32[]{:S(2)}) collective-permute-start(f32[1,16,1,128]{3,2,1,0:T(1,128)S(1)} %slice.335), channel_id=1, source_target_pairs={{8,0},{16,8},{24,16},{32,24},{40,32},{48,40},{56,48},{64,56},{72,6... | collective-permute-start | bytes 24584 | tf_op jit(solution)/shard_map/ppermute | solution.py:12
  20.3 5.4 %collective-permute-start.6 = (f32[1,16,64,1]{3,2,1,0:T(8,128)S(1)}, f32[1,16,64,1]{3,2,1,0:T(8,128)S(1)}, u32[]{:S(2)}, u32[]{:S(2)}) collective-permute-start(f32[1,16,64,1]{3,2,1,0:T(8,128)S(1)} %bitcast.123), channel_id=1, source_target_pairs={{4,0},{5,1},{6,2},{7,3},{12,8},{13,9},{14,10},{15,11},{20,16},{21,... | collective-permute-start | bytes 12296 | tf_op jit(solution)/shard_map/ppermute | solution.py:12
  26.3 6.0 %collective-permute-start.7 = (f32[1,16,64,1]{3,2,1,0:T(8,128)S(1)}, f32[1,16,64,1]{3,2,1,0:T(8,128)S(1)}, u32[]{:S(2)}, u32[]{:S(2)}) collective-permute-start(f32[1,16,64,1]{3,2,1,0:T(8,128)S(1)} %slice.340), channel_id=1, source_target_pairs={{0,4},{1,5},{2,6},{3,7},{8,12},{9,13},{10,14},{11,15},{16,20},{17,... | collective-permute-start | bytes 12296 | tf_op jit(solution)/shard_map/ppermute | solution.py:12
  27.6 5.3 %collective-permute-start.5 = (f32[1,16,1,128]{3,2,1,0:T(1,128)S(1)}, f32[1,16,1,128]{3,2,1,0:T(1,128)S(1)}, u32[]{:S(2)}, u32[]{:S(2)}) collective-permute-start(f32[1,16,1,128]{3,2,1,0:T(1,128)S(1)} %slice.336), channel_id=1, source_target_pairs={{0,8},{8,16},{16,24},{24,32},{32,40},{40,48},{48,56},{56,64},{64,7... | collective-permute-start | bytes 24584 | tf_op jit(solution)/shard_map/ppermute | solution.py:12
  33.5 6.9 %collective-permute-start.8 = (f32[1,16,1,128]{3,2,1,0:T(1,128)S(1)}, f32[1,16,1,128]{3,2,1,0:T(1,128)S(1)}, u32[]{:S(2)}, u32[]{:S(2)}) collective-permute-start(f32[1,16,1,128]{3,2,1,0:T(1,128)S(1)} %slice.345), channel_id=1, source_target_pairs={{8,0},{16,8},{24,16},{32,24},{40,32},{48,40},{56,48},{64,56},{72,6... | collective-permute-start | bytes 24584 | tf_op jit(solution)/shard_map/ppermute | solution.py:12
  34.8 5.6 %collective-permute-start.10 = (f32[1,16,64,1]{3,2,1,0:T(8,128)S(1)}, f32[1,16,64,1]{3,2,1,0:T(8,128)}, u32[]{:S(2)}, u32[]{:S(2)}) collective-permute-start(f32[1,16,64,1]{3,2,1,0:T(8,128)S(1)} %bitcast.124), channel_id=1, source_target_pairs={{4,0},{5,1},{6,2},{7,3},{12,8},{13,9},{14,10},{15,11},{20,16},{21,... | collective-permute-start | bytes 12296 | tf_op jit(solution)/shard_map/ppermute | solution.py:12
  42.0 5.9 %collective-permute-start.11 = (f32[1,16,64,1]{3,2,1,0:T(8,128)S(1)}, f32[1,16,64,1]{3,2,1,0:T(8,128)S(1)}, u32[]{:S(2)}, u32[]{:S(2)}) collective-permute-start(f32[1,16,64,1]{3,2,1,0:T(8,128)S(1)} %slice.350), channel_id=1, source_target_pairs={{0,4},{1,5},{2,6},{3,7},{8,12},{9,13},{10,14},{11,15},{16,20},{17,... | collective-permute-start | bytes 12296 | tf_op jit(solution)/shard_map/ppermute | solution.py:12
  43.3 5.3 %collective-permute-start.9 = (f32[1,16,1,128]{3,2,1,0:T(1,128)S(1)}, f32[1,16,1,128]{3,2,1,0:T(1,128)S(1)}, u32[]{:S(2)}, u32[]{:S(2)}) collective-permute-start(f32[1,16,1,128]{3,2,1,0:T(1,128)S(1)} %slice.346), channel_id=1, source_target_pairs={{0,8},{8,16},{16,24},{24,32},{32,40},{40,48},{48,56},{56,64},{64,7... | collective-permute-start | bytes 24584 | tf_op jit(solution)/shard_map/ppermute | solution.py:12
  48.7 5.9 %copy-start.5 = (s32[1,4096]{1,0:T(1,128)S(1)}, s32[1,4096]{1,0:T(1,128)}, u32[]{:S(2)}) copy-start(s32[1,4096]{1,0:T(1,128)} %param.12) | copy-start | bytes 49156
  49.3 5.5 %collective-permute-start.14 = (f32[1,16,64,1]{3,2,1,0:T(8,128)S(1)}, f32[1,16,64,1]{3,2,1,0:T(8,128)S(1)}, u32[]{:S(2)}, u32[]{:S(2)}) collective-permute-start(f32[1,16,64,1]{3,2,1,0:T(8,128)S(1)} %bitcast.125), channel_id=1, source_target_pairs={{4,0},{5,1},{6,2},{7,3},{12,8},{13,9},{14,10},{15,11},{20,16},{21,... | collective-permute-start | bytes 12296 | tf_op jit(solution)/shard_map/ppermute | solution.py:12
  53.3 4.9 %collective-permute-start.12 = (f32[1,16,1,128]{3,2,1,0:T(1,128)S(1)}, f32[1,16,1,128]{3,2,1,0:T(1,128)S(1)}, u32[]{:S(2)}, u32[]{:S(2)}) collective-permute-start(f32[1,16,1,128]{3,2,1,0:T(1,128)S(1)} %slice.355), channel_id=1, source_target_pairs={{8,0},{16,8},{24,16},{32,24},{40,32},{48,40},{56,48},{64,56},{72,6... | collective-permute-start | bytes 24584 | tf_op jit(solution)/shard_map/ppermute | solution.py:12
  58.8 6.5 %collective-permute-start.15 = (f32[1,16,64,1]{3,2,1,0:T(8,128)S(1)}, f32[1,16,64,1]{3,2,1,0:T(8,128)S(1)}, u32[]{:S(2)}, u32[]{:S(2)}) collective-permute-start(f32[1,16,64,1]{3,2,1,0:T(8,128)S(1)} %slice.360), channel_id=1, source_target_pairs={{0,4},{1,5},{2,6},{3,7},{8,12},{9,13},{10,14},{11,15},{16,20},{17,... | collective-permute-start | bytes 12296 | tf_op jit(solution)/shard_map/ppermute | solution.py:12
  60.1 5.8 %collective-permute-start.13 = (f32[1,16,1,128]{3,2,1,0:T(1,128)S(1)}, f32[1,16,1,128]{3,2,1,0:T(1,128)S(1)}, u32[]{:S(2)}, u32[]{:S(2)}) collective-permute-start(f32[1,16,1,128]{3,2,1,0:T(1,128)S(1)} %slice.356), channel_id=1, source_target_pairs={{0,8},{8,16},{16,24},{24,32},{32,40},{40,48},{48,56},{56,64},{64,7... | collective-permute-start | bytes 24584 | tf_op jit(solution)/shard_map/ppermute | solution.py:12
  66.6 5.5 %collective-permute-start.18 = (f32[1,16,64,1]{3,2,1,0:T(8,128)S(1)}, f32[1,16,64,1]{3,2,1,0:T(8,128)S(1)}, u32[]{:S(2)}, u32[]{:S(2)}) collective-permute-start(f32[1,16,64,1]{3,2,1,0:T(8,128)S(1)} %bitcast.126), channel_id=1, source_target_pairs={{4,0},{5,1},{6,2},{7,3},{12,8},{13,9},{14,10},{15,11},{20,16},{21,... | collective-permute-start | bytes 12296 | tf_op jit(solution)/shard_map/ppermute | solution.py:12
  70.5 5.8 %collective-permute-start.16 = (f32[1,16,1,128]{3,2,1,0:T(1,128)S(1)}, f32[1,16,1,128]{3,2,1,0:T(1,128)S(1)}, u32[]{:S(2)}, u32[]{:S(2)}) collective-permute-start(f32[1,16,1,128]{3,2,1,0:T(1,128)S(1)} %slice.365), channel_id=1, source_target_pairs={{8,0},{16,8},{24,16},{32,24},{40,32},{48,40},{56,48},{64,56},{72,6... | collective-permute-start | bytes 24584 | tf_op jit(solution)/shard_map/ppermute | solution.py:12
  76.8 7.5 %collective-permute-start.19 = (f32[1,16,64,1]{3,2,1,0:T(8,128)S(1)}, f32[1,16,64,1]{3,2,1,0:T(8,128)S(1)}, u32[]{:S(2)}, u32[]{:S(2)}) collective-permute-start(f32[1,16,64,1]{3,2,1,0:T(8,128)S(1)} %slice.370), channel_id=1, source_target_pairs={{0,4},{1,5},{2,6},{3,7},{8,12},{9,13},{10,14},{11,15},{16,20},{17,... | collective-permute-start | bytes 12296 | tf_op jit(solution)/shard_map/ppermute | solution.py:12
  78.1 6.8 %collective-permute-start.17 = (f32[1,16,1,128]{3,2,1,0:T(1,128)S(1)}, f32[1,16,1,128]{3,2,1,0:T(1,128)S(1)}, u32[]{:S(2)}, u32[]{:S(2)}) collective-permute-start(f32[1,16,1,128]{3,2,1,0:T(1,128)S(1)} %slice.366), channel_id=1, source_target_pairs={{0,8},{8,16},{16,24},{24,32},{32,40},{40,48},{48,56},{56,64},{64,7... | collective-permute-start | bytes 24584 | tf_op jit(solution)/shard_map/ppermute | solution.py:12
  84.9 5.9 %copy-start.6 = (s32[1,128]{1,0:T(1,128)S(1)}, s32[1,128]{1,0:T(1,128)}, u32[]{:S(2)}) copy-start(s32[1,128]{1,0:T(1,128)} %param.13) | copy-start | bytes 1540
  85.6 5.7 %collective-permute-start.22 = (f32[1,16,64,1]{3,2,1,0:T(8,128)S(1)}, f32[1,16,64,1]{3,2,1,0:T(8,128)S(1)}, u32[]{:S(2)}, u32[]{:S(2)}) collective-permute-start(f32[1,16,64,1]{3,2,1,0:T(8,128)S(1)} %bitcast.127), channel_id=1, source_target_pairs={{4,0},{5,1},{6,2},{7,3},{12,8},{13,9},{14,10},{15,11},{20,16},{21,... | collective-permute-start | bytes 12296 | tf_op jit(solution)/shard_map/ppermute | solution.py:12
  89.5 4.9 %collective-permute-start.20 = (f32[1,16,1,128]{3,2,1,0:T(1,128)S(1)}, f32[1,16,1,128]{3,2,1,0:T(1,128)S(1)}, u32[]{:S(2)}, u32[]{:S(2)}) collective-permute-start(f32[1,16,1,128]{3,2,1,0:T(1,128)S(1)} %slice.375), channel_id=1, source_target_pairs={{8,0},{16,8},{24,16},{32,24},{40,32},{48,40},{56,48},{64,56},{72,6... | collective-permute-start | bytes 24584 | tf_op jit(solution)/shard_map/ppermute | solution.py:12
  95.0 7.0 %collective-permute-start.23 = (f32[1,16,64,1]{3,2,1,0:T(8,128)S(1)}, f32[1,16,64,1]{3,2,1,0:T(8,128)S(1)}, u32[]{:S(2)}, u32[]{:S(2)}) collective-permute-start(f32[1,16,64,1]{3,2,1,0:T(8,128)S(1)} %slice.380), channel_id=1, source_target_pairs={{0,4},{1,5},{2,6},{3,7},{8,12},{9,13},{10,14},{11,15},{16,20},{17,... | collective-permute-start | bytes 12296 | tf_op jit(solution)/shard_map/ppermute | solution.py:12
  96.4 6.4 %collective-permute-start.21 = (f32[1,16,1,128]{3,2,1,0:T(1,128)S(1)}, f32[1,16,1,128]{3,2,1,0:T(1,128)S(1)}, u32[]{:S(2)}, u32[]{:S(2)}) collective-permute-start(f32[1,16,1,128]{3,2,1,0:T(1,128)S(1)} %slice.376), channel_id=1, source_target_pairs={{0,8},{8,16},{16,24},{24,32},{32,40},{40,48},{48,56},{56,64},{64,7... | collective-permute-start | bytes 24584 | tf_op jit(solution)/shard_map/ppermute | solution.py:12
  103.4 5.5 %collective-permute-start.26 = (f32[1,16,64,1]{3,2,1,0:T(8,128)S(1)}, f32[1,16,64,1]{3,2,1,0:T(8,128)S(1)}, u32[]{:S(2)}, u32[]{:S(2)}) collective-permute-start(f32[1,16,64,1]{3,2,1,0:T(8,128)S(1)} %bitcast.128), channel_id=1, source_target_pairs={{4,0},{5,1},{6,2},{7,3},{12,8},{13,9},{14,10},{15,11},{20,16},{21,... | collective-permute-start | bytes 12296 | tf_op jit(solution)/shard_map/ppermute | solution.py:12
  107.3 4.9 %collective-permute-start.24 = (f32[1,16,1,128]{3,2,1,0:T(1,128)S(1)}, f32[1,16,1,128]{3,2,1,0:T(1,128)S(1)}, u32[]{:S(2)}, u32[]{:S(2)}) collective-permute-start(f32[1,16,1,128]{3,2,1,0:T(1,128)S(1)} %slice.385), channel_id=1, source_target_pairs={{8,0},{16,8},{24,16},{32,24},{40,32},{48,40},{56,48},{64,56},{72,6... | collective-permute-start | bytes 24584 | tf_op jit(solution)/shard_map/ppermute | solution.py:12
  112.8 7.2 %collective-permute-start.27 = (f32[1,16,64,1]{3,2,1,0:T(8,128)S(1)}, f32[1,16,64,1]{3,2,1,0:T(8,128)S(1)}, u32[]{:S(2)}, u32[]{:S(2)}) collective-permute-start(f32[1,16,64,1]{3,2,1,0:T(8,128)S(1)} %slice.390), channel_id=1, source_target_pairs={{0,4},{1,5},{2,6},{3,7},{8,12},{9,13},{10,14},{11,15},{16,20},{17,... | collective-permute-start | bytes 12296 | tf_op jit(solution)/shard_map/ppermute | solution.py:12
  114.3 6.4 %collective-permute-start.25 = (f32[1,16,1,128]{3,2,1,0:T(1,128)S(1)}, f32[1,16,1,128]{3,2,1,0:T(1,128)S(1)}, u32[]{:S(2)}, u32[]{:S(2)}) collective-permute-start(f32[1,16,1,128]{3,2,1,0:T(1,128)S(1)} %slice.386), channel_id=1, source_target_pairs={{0,8},{8,16},{16,24},{24,32},{32,40},{40,48},{48,56},{56,64},{64,7... | collective-permute-start | bytes 24584 | tf_op jit(solution)/shard_map/ppermute | solution.py:12
  121.3 7.4 %collective-permute-start.30 = (f32[1,16,64,1]{3,2,1,0:T(8,128)S(1)}, f32[1,16,64,1]{3,2,1,0:T(8,128)S(1)}, u32[]{:S(2)}, u32[]{:S(2)}) collective-permute-start(f32[1,16,64,1]{3,2,1,0:T(8,128)S(1)} %bitcast.129), channel_id=1, source_target_pairs={{4,0},{5,1},{6,2},{7,3},{12,8},{13,9},{14,10},{15,11},{20,16},{21,... | collective-permute-start | bytes 12296 | tf_op jit(solution)/shard_map/ppermute | solution.py:12
  125.3 4.9 %collective-permute-start.28 = (f32[1,16,1,128]{3,2,1,0:T(1,128)S(1)}, f32[1,16,1,128]{3,2,1,0:T(1,128)S(1)}, u32[]{:S(2)}, u32[]{:S(2)}) collective-permute-start(f32[1,16,1,128]{3,2,1,0:T(1,128)S(1)} %slice.395), channel_id=1, source_target_pairs={{8,0},{16,8},{24,16},{32,24},{40,32},{48,40},{56,48},{64,56},{72,6... | collective-permute-start | bytes 24584 | tf_op jit(solution)/shard_map/ppermute | solution.py:12
  130.8 7.0 %collective-permute-start.31 = (f32[1,16,64,1]{3,2,1,0:T(8,128)S(1)}, f32[1,16,64,1]{3,2,1,0:T(8,128)S(1)}, u32[]{:S(2)}, u32[]{:S(2)}) collective-permute-start(f32[1,16,64,1]{3,2,1,0:T(8,128)S(1)} %slice.400), channel_id=1, source_target_pairs={{0,4},{1,5},{2,6},{3,7},{8,12},{9,13},{10,14},{11,15},{16,20},{17,... | collective-permute-start | bytes 12296 | tf_op jit(solution)/shard_map/ppermute | solution.py:12
  132.1 6.4 %collective-permute-start.29 = (f32[1,16,1,128]{3,2,1,0:T(1,128)S(1)}, f32[1,16,1,128]{3,2,1,0:T(1,128)S(1)}, u32[]{:S(2)}, u32[]{:S(2)}) collective-permute-start(f32[1,16,1,128]{3,2,1,0:T(1,128)S(1)} %slice.396), channel_id=1, source_target_pairs={{0,8},{8,16},{16,24},{24,32},{32,40},{40,48},{48,56},{56,64},{64,7... | collective-permute-start | bytes 24584 | tf_op jit(solution)/shard_map/ppermute | solution.py:12
where the time goes:
time: 186 us; the launch traced here: 185 us
  starting transfers between devices  95.4 us (51%)
  blocking collectives  42.1 us (23%)
  waiting for transfers between devices  23.4 us (13%)
  other arithmetic  12.1 us (7%)
  local copies, waits for them, and re-layouts  9.92 us (5%)
    ppermute x32, starting transfers between devices, from_behind(): return lax.ppermute(shard, axis, pairs)  95.4 us
    all_to_all x1, blocking collectives, shards(): lax.all_to_all(outgoing, ('along', 'cross'), split_axis=0, concat_axis=0,...  42.1 us
    ppermute x32, waiting for transfers between devices, from_behind(): return lax.ppermute(shard, axis, pairs)  23.4 us
    mul x7, other arithmetic, run_steps(): wet_mask * (pressure - stiffness * (flow_along - behind + (flow_cross - b...  4.42 us
  transfers between devices with their start and end apart: 32, of which 16 were waited for; matrix products, arithmetic and copies ran while one was open for 4% of the time, Pallas kernels for 0%

commit v1 on v0

v1 whole, which is shorter than its diff:
```python
import functools

import jax
import jax.numpy as jnp
from jax import lax
from jax.experimental import pallas as pl
from jax.experimental.pallas import tpu as pltpu
from jax.sharding import PartitionSpec as P

STEPS = 8
HALO = 8
PAD = 8
MESH = pl.DeviceIdType.MESH


def kernel(
    n_along,
    layers,
    rows,
    cols,
    cap,
    p_hbm,
    fa_hbm,
    fc_hbm,
    d_hbm,
    k_hbm,
    lists_hbm,
    owners_hbm,
    out_p,
    out_s,
    ep,
    ea,
    ec,
    dx,
    kx,
    lists,
    owners,
    place,
    trace,
    trace_out,
    outgoing,
    local_sem,
    halo_send,
    halo_recv,
    trace_send,
    trace_recv,
    panel_send,
    panel_recv,
    final_sem,
):
    i = lax.axis_index("along")
    j = lax.axis_index("cross")
    other = 1 - j
    block = i * 2 + j
    n_owners = 2 * n_along
    half = rows // 2
    ext = half + HALO
    slots = n_owners * cap

    list_copy = pltpu.make_async_copy(lists_hbm, lists, local_sem.at[5])
    owner_copy = pltpu.make_async_copy(owners_hbm, owners, local_sem.at[6])
    list_copy.start()
    owner_copy.start()
    fields = ((p_hbm, ep), (fa_hbm, ea), (fc_hbm, ec), (d_hbm, dx), (k_hbm, kx))

    def take(src, start, count):
        if len(src.shape) == 4:
            return src.at[0, :, pl.ds(start, count), :]
        return src.at[pl.ds(start, count), :]

    def put(dst, side, start, count):
        if len(dst.shape) == 4:
            return dst.at[side, :, pl.ds(start, count), :]
        return dst.at[side, pl.ds(start, count), :]

    def first_row(core):
        return pl.multiple_of((half - HALO) * core, 8)

    def first_slot(core):
        return pl.multiple_of(PAD + HALO - HALO * core, 8)

    own_copies = []
    for index, (src, dst) in enumerate(fields):
        copy = pltpu.make_async_copy(
            take(src, first_row(j), ext), put(dst, j, first_slot(j), ext), local_sem.at[index]
        )
        copy.start()
        own_copies.append(copy)

    barrier = pltpu.get_barrier_semaphore()

    def greet(k, carry):
        o = lax.rem(block + k, n_owners)
        pl.semaphore_signal(
            barrier, inc=1, device_id={"along": o // 2, "cross": lax.rem(o, 2)}, device_id_type=MESH
        )
        return carry

    lax.fori_loop(1, n_owners, greet, 0)

    for index, (src, dst) in enumerate(fields):
        if len(dst.shape) == 4:
            tail = PAD + ext + HALO
            dst[:, :, 0:PAD, :] = jnp.zeros((2, layers, PAD, cols), jnp.float32)
            dst[:, :, tail : tail + PAD, :] = jnp.zeros((2, layers, PAD, cols), jnp.float32)

    list_copy.wait()
    owner_copy.wait()
    patches = 2 * rows
    lane_r = lax.broadcasted_iota(jnp.int32, (patches, patches), 0)
    lane_c = lax.broadcasted_iota(jnp.int32, (patches, patches), 1)
    id_r = 2 * lax.rem(lane_r, rows) + lane_r // rows
    id_c = 2 * lax.rem(lane_c, rows) + lane_c // rows
    wanted = id_r + block * patches
    seen = jnp.zeros((patches, lists.shape[1]), jnp.float32)
    for row in range(lists.shape[0]):
        seen = jnp.where(lists[row : row + 1, :] == wanted, 1.0, seen)
    ones = jnp.ones((8, lists.shape[1]), jnp.bfloat16)
    member = lax.dot_general(
        ones, seen.astype(jnp.bfloat16), (((1,), (1,)), ((), ())), preferred_element_type=jnp.float32
    )
    permute = jnp.where(lane_r == id_c, 1.0, 0.0).astype(jnp.bfloat16)
    owner_rows = jnp.broadcast_to(owners[...].astype(jnp.float32), (8, patches)).astype(jnp.bfloat16)
    owner_of = jnp.dot(owner_rows, permute, preferred_element_type=jnp.float32)
    slot = lax.broadcasted_iota(jnp.int32, (slots, patches), 0)
    slot_owner = slot // cap
    slot_rank = (slot - slot_owner * cap).astype(jnp.float32)
    mine = owner_of[0:1, :] == slot_owner.astype(jnp.float32)
    before = jnp.where(id_r < id_c, 1.0, 0.0).astype(jnp.bfloat16)
    rank = jnp.dot(
        jnp.where(mine, 1.0, 0.0).astype(jnp.bfloat16), before, preferred_element_type=jnp.float32
    )
    held = jnp.where(mine & (rank == slot_rank), jnp.where(member[0:1, :] > 0.5, 1.0, 0.0), 0.0)
    place[...] = held.astype(jnp.bfloat16)

    pl.semaphore_wait(barrier, n_owners - 1)

    after_chip = lax.rem(i + 1, n_along)
    before_chip = lax.rem(i + n_along - 1, n_along)
    sends = []
    for index, (src, dst) in enumerate(fields):
        sends.append(
            pltpu.make_async_remote_copy(
                src_ref=take(src, rows - HALO, HALO),
                dst_ref=put(dst, j, PAD, HALO),
                send_sem=halo_send.at[index, 0],
                recv_sem=halo_recv.at[index, 1 + j],
                device_id={"along": after_chip, "cross": 0},
                device_id_type=MESH,
            )
        )
        sends.append(
            pltpu.make_async_remote_copy(
                src_ref=take(src, 0, HALO),
                dst_ref=put(dst, j, PAD + ext, HALO),
                send_sem=halo_send.at[index, 1],
                recv_sem=halo_recv.at[index, 1 + j],
                device_id={"along": before_chip, "cross": 1},
                device_id_type=MESH,
            )
        )
        sends.append(
            pltpu.make_async_remote_copy(
                src_ref=take(src, first_row(other), ext),
                dst_ref=put(dst, j, first_slot(other), ext),
                send_sem=halo_send.at[index, 2],
                recv_sem=halo_recv.at[index, 0],
                device_id={"cross": other},
                device_id_type=MESH,
            )
        )
    for copy in sends:
        copy.start()
    for copy in own_copies:
        copy.wait()
    for index, (src, dst) in enumerate(fields):
        for source in range(3):
            count = ext if source == 0 else HALO
            pltpu.make_async_copy(
                take(src, 0, count), put(dst, 0, PAD, count), halo_recv.at[index, source]
            ).wait()

    @pl.when((i == 0) & (j == 0))
    def _():
        ep[:, :, PAD : PAD + HALO, :] = jnp.zeros((2, layers, HALO, cols), jnp.float32)
        dx[:, PAD : PAD + HALO, :] = jnp.zeros((2, HALO, cols), jnp.int32)

    @pl.when((i == n_along - 1) & (j == 1))
    def _():
        ep[:, :, PAD + ext : PAD + ext + HALO, :] = jnp.zeros((2, layers, HALO, cols), jnp.float32)
        dx[:, PAD + ext : PAD + ext + HALO, :] = jnp.zeros((2, HALO, cols), jnp.int32)

    lane = lax.broadcasted_iota(jnp.int32, (8, cols), 1)
    first_lane = lane == 0
    last_lane = lane == cols - 1
    low_lanes = lax.broadcasted_iota(jnp.int32, (rows, cols), 1) < cols // 2
    zero = jnp.zeros((8, cols), jnp.float32)
    tiles = (half + 2 * HALO) // 8
    own_tiles = range(HALO // 8, HALO // 8 + half // 8)
    own_start = pl.multiple_of(half * j, 8)

    def trace_copy(t):
        return pltpu.make_async_remote_copy(
            src_ref=trace_out.at[t],
            dst_ref=trace.at[t, pl.ds(own_start, half), :],
            send_sem=trace_send.at[t],
            recv_sem=trace_recv.at[t],
            device_id={"cross": other},
            device_id_type=MESH,
        )

    def step(t):
        for tile in range(tiles):
            r = PAD + 8 * tile
            depth = [dx[h, r : r + 8, :] for h in range(2)]
            stiff = [kx[h, r : r + 8, :] for h in range(2)]
            half_stiff = [0.5 * stiff[h] for h in range(2)]
            pressure = [ep[h, 0, r : r + 8, :] for h in range(2)]
            wet = [depth[h] > 0 for h in range(2)]
            down = [zero, zero]
            seafloor = [zero, zero]
            for z in range(layers):
                turned = [pltpu.roll(pressure[h], cols - 1, 1) for h in range(2)]
                right = [
                    jnp.where(last_lane, turned[1], turned[0]),
                    jnp.where(last_lane, 0.0, turned[1]),
                ]
                along = []
                cross = []
                for h in range(2):
                    ahead = ep[h, z, r + 1 : r + 9, :]
                    value = jnp.where(wet[h], ea[h, z, r : r + 8, :] - (ahead - pressure[h]), 0.0)
                    ea[h, z, r : r + 8, :] = value
                    along.append(value)
                    value = jnp.where(
                        wet[h], ec[h, z, r : r + 8, :] - (right[h] - pressure[h]), 0.0
                    )
                    ec[h, z, r : r + 8, :] = value
                    cross.append(value)
                turned = [pltpu.roll(cross[h], 1, 1) for h in range(2)]
                left = [
                    jnp.where(first_lane, 0.0, turned[0]),
                    jnp.where(first_lane, turned[0], turned[1]),
                ]
                for h in range(2):
                    behind = ea[h, z, r - 1 : r + 7, :]
                    spread = (along[h] - behind) + (cross[h] - left[h])
                    if z + 1 < layers:
                        lower = ep[h, z + 1, r : r + 8, :]
                        wet_lower = depth[h] > z + 1
                        up = jnp.where(wet_lower, lower - pressure[h], 0.0)
                        vertical = up - down[h]
                    else:
                        vertical = -down[h]
                    value = pressure[h] - stiff[h] * spread + half_stiff[h] * vertical
                    value = jnp.where(wet[h], value, 0.0)
                    ep[h, z, r : r + 8, :] = value
                    seafloor[h] = jnp.where(wet[h], value, seafloor[h])
                    if z + 1 < layers:
                        pressure[h] = lower
                        wet[h] = wet_lower
                        down[h] = up
            if tile in own_tiles:
                at = 8 * (tile - HALO // 8)
                trace[t, pl.ds(pl.multiple_of(own_start + at, 8), 8), :] = jnp.where(
                    j == 0, seafloor[0], seafloor[1]
                )
                trace_out[t, at : at + 8, :] = jnp.where(j == 0, seafloor[1], seafloor[0])
        trace_copy(t).start()

    def panel_copy(g, k):
        o = lax.rem(block + k, n_owners)
        return pltpu.make_async_remote_copy(
            src_ref=outgoing.at[g, pl.ds(o * cap, cap)],
            dst_ref=out_s.at[pl.ds(block * cap, cap), g],
            send_sem=panel_send.at[g],
            recv_sem=panel_recv.at[g],
            device_id={"along": o // 2, "cross": lax.rem(o, 2)},
            device_id_type=MESH,
        )

    def own_panel_copy(g):
        return pltpu.make_async_copy(
            outgoing.at[g, pl.ds(block * cap, cap)],
            out_s.at[pl.ds(block * cap, cap), g],
            final_sem.at[2 + g],
        )

    def send_group(g):
        pair = []
        for s in range(2):
            trace_copy(2 * g + s).wait_recv()
        first, second = trace[2 * g], trace[2 * g + 1]
        left = jnp.where(low_lanes, first, pltpu.roll(second, cols // 2, 1))
        right = jnp.where(low_lanes, pltpu.roll(first, cols // 2, 1), second)
        rest = jnp.concatenate([left, right], 0)
        total = None
        for part in range(3):
            piece = rest.astype(jnp.bfloat16)
            term = jnp.dot(place[...], piece, preferred_element_type=jnp.float32)
            total = term if total is None else total + term
            rest = rest - piece.astype(jnp.float32)
        outgoing[g, :, 0, :] = total
        own_panel_copy(g).start()

        def send(k, carry):
            panel_copy(g, k).start()
            return carry

        lax.fori_loop(1, n_owners, send, 0)

    own_pressure = pltpu.make_async_copy(
        ep.at[j, :, pl.ds(PAD + HALO, half), :],
        out_p.at[0, :, pl.ds(own_start, half), :],
        final_sem.at[0],
    )
    other_pressure = pltpu.make_async_remote_copy(
        src_ref=ep.at[other, :, pl.ds(PAD + HALO, half), :],
        dst_ref=out_p.at[0, :, pl.ds(own_start, half), :],
        send_sem=final_sem.at[1],
        recv_sem=final_sem.at[6],
        device_id={"cross": other},
        device_id_type=MESH,
    )

    def advance(t, carry):
        @pl.when(t < STEPS)
        def _():
            step(t)

        @pl.when(t == STEPS - 1)
        def _():
            own_pressure.start()
            other_pressure.start()

        @pl.when((t >= 2) & (lax.rem(t, 2) == 0))
        def _():
            send_group(t // 2 - 1)

        return carry

    lax.fori_loop(0, STEPS + 1, advance, 0)

    for copy in sends:
        copy.wait_send()
    for t in range(STEPS):
        trace_copy(t).wait_send()
    own_pressure.wait()
    other_pressure.wait()
    moved = (n_owners - 1) * cap
    for g in range(STEPS // 2):
        own_panel_copy(g).wait()
        pltpu.make_async_copy(
            outgoing.at[g, pl.ds(0, moved)], out_s.at[pl.ds(0, moved), g], panel_send.at[g]
        ).wait()
        pltpu.make_async_copy(
            outgoing.at[g, pl.ds(0, moved)], out_s.at[pl.ds(0, moved), g], panel_recv.at[g]
        ).wait()


def shards(
    pressure_start, along_start, cross_start, depth_layers, stiffness, patch_lists, owner_map
):
    _, layers, rows, cols = pressure_start.shape
    n_along = lax.axis_size("along")
    n_owners = n_along * lax.axis_size("cross")
    cap = 2 * rows // n_owners + 1
    slots = n_owners * cap
    ext_rows = rows // 2 + 2 * HALO + 2 * PAD
    lists = patch_lists.reshape(-1, cols)
    any_space = pl.BlockSpec(memory_space=pl.ANY)
    pressure, panels = pl.pallas_call(
        functools.partial(kernel, n_along, layers, rows, cols, cap),
        out_shape=(
            jax.ShapeDtypeStruct(pressure_start.shape, jnp.float32),
            jax.ShapeDtypeStruct((slots, STEPS // 2, 1, cols), jnp.float32),
        ),
        in_specs=[any_space] * 7,
        out_specs=(any_space, any_space),
        scratch_shapes=[
            pltpu.VMEM((2, layers, ext_rows, cols), jnp.float32),
            pltpu.VMEM((2, layers, ext_rows, cols), jnp.float32),
            pltpu.VMEM((2, layers, ext_rows, cols), jnp.float32),
            pltpu.VMEM((2, ext_rows, cols), jnp.int32),
            pltpu.VMEM((2, ext_rows, cols), jnp.float32),
            pltpu.VMEM(lists.shape, jnp.int32),
            pltpu.VMEM(owner_map.shape, jnp.int32),
            pltpu.VMEM((slots, 2 * rows), jnp.bfloat16),
            pltpu.VMEM((STEPS, rows, cols), jnp.float32),
            pltpu.VMEM((STEPS, rows // 2, cols), jnp.float32),
            pltpu.VMEM((STEPS // 2, slots, 1, cols), jnp.float32),
            pltpu.SemaphoreType.DMA((7,)),
            pltpu.SemaphoreType.DMA((5, 3)),
            pltpu.SemaphoreType.DMA((5, 3)),
            pltpu.SemaphoreType.DMA((STEPS,)),
            pltpu.SemaphoreType.DMA((STEPS,)),
            pltpu.SemaphoreType.DMA((STEPS // 2,)),
            pltpu.SemaphoreType.DMA((STEPS // 2,)),
            pltpu.SemaphoreType.DMA((7,)),
        ],
        compiler_params=pltpu.CompilerParams(collective_id=0, has_side_effects=True),
    )(
        pressure_start,
        along_start,
        cross_start,
        depth_layers,
        stiffness,
        lists,
        owner_map,
    )
    return (pressure, panels.reshape(1, slots, 1, STEPS // 2 * cols))


def solution(mesh):
    in_specs = (
        P("batch", None, "along", "cross"),
        P("batch", None, "along", "cross"),
        P("batch", None, "along", "cross"),
        P("along", "cross"),
        P("along", "cross"),
        P("batch", None),
        P(("along", "cross"), None),
    )
    out_specs = (P("batch", None, "along", "cross"), P(("along", "cross"), None, "batch", None))
    return jax.shard_map(shards, mesh=mesh, in_specs=in_specs, out_specs=out_specs, check_vma=False)
```

time: 186 us -> 74.6 us (0.40)
  starting transfers between devices: 95.4 us -> 0 us
  Pallas kernels: 0 us -> 71.2 us
  blocking collectives: 42.1 us -> 0 us
  waiting for transfers between devices: 23.4 us -> 0 us
  other arithmetic: 12.1 us -> 0 us
  local copies, waits for them, and re-layouts: 9.92 us -> 2.68 us
    ppermute x32 -> x0, starting transfers between devices: 95.4 us -> none  [from_behind(): return lax.ppermute(shard, axis, pairs)]
    pallas_call x0 -> x1, Pallas kernels: none -> 71.2 us  [shards(): pl.pallas_call(functools.partial(kernel, n_along, layers, rows, cols, cap...]
    all_to_all x1 -> x0, blocking collectives: 42.1 us -> none  [shards(): lax.all_to_all(outgoing, ('along', 'cross'), split_axis=0, concat_axis=0,...]
    ppermute x32 -> x0, waiting for transfers between devices: 23.4 us -> none  [from_behind(): return lax.ppermute(shard, axis, pairs)]
    mul x16 -> x0, other arithmetic: 8.21 us -> none  [the longest x7 4.42 us: run_steps(): wet_mask * (pressure - stiffness * (flow_along - behind + (flow_cross - b...]
    slice x49 -> x0, local copies, waits for them, and re-layouts: 6.56 us -> none  [the longest x8 1.85 us: run_steps(): upper_layer = jnp.concatenate([zero_sensor_layer, pressure[:, :-1]], 1)]
    reduce_sum x2 -> x0, other arithmetic: 1.88 us -> none  [the longest x1 1.71 us: run_steps(): traces.append(jnp.sum(pressure * onehot, axis=1))]
    reduce_or x1 -> x0, other arithmetic: 1.87 us -> none  [shards(): jnp.any(local_ids[:, :, None] == positions[None, None, :], axis=1)]
  transfers between devices with their start and end apart: 32 -> 0, of which waited for: 16 -> 0; matrix products, arithmetic and copies ran while one was open for 4% -> 0% of each run, Pallas kernels for 0% -> 0%
where the time goes in v1:
time: 74.6 us; the launch traced here: 74.5 us
  Pallas kernels  71.2 us (95%)
  local copies, waits for them, and re-layouts  2.68 us (4%)
    pallas_call x1, Pallas kernels, shards(): pl.pallas_call(functools.partial(kernel, n_along, layers, rows, cols, cap...  71.2 us
    unnamed x4, local copies, waits for them, and re-layouts  2.68 us

profile of v1, /device:TPU:1, one launch (start us, length us, event | category | flops | bytes accessed | tf_op | source)
XLA Modules:
  0.0 74.5 jit_solution(16658687865530360088)
XLA Ops:
  0.6 71.2 %shard_map.86 = (f32[1,16,64,128]{3,2,1,0:T(8,128)}, f32[192,4,1,128]{3,2,1,0:T(1,128)}) custom-call(f32[1,16,64,128]{3,2,1,0:T(8,128)} %p_hbm.1, f32[1,16,64,128]{3,2,1,0:T(8,128)} %fa_hbm.1, f32[1,16,64,128]{3,2,1,0:T(8,128)} %fc_hbm.1, s32[64,128]{1,0:T(8,128)} %d_hbm.1, f32[64,128]{1,0:T(8,128)} %k_hbm.1, s32[32,128]{1,0:T(8,128)} %bitcast.3, ...), custom_call_target="tpu_custom_call" | custom-call | tf_op jit(solution)/shard_map/pallas_call | solution.py:372
  71.8 0.0 copy-start
  71.8 1.9 %copy.12 = f32[1,16,64,128]{3,2,1,0:T(8,128)} copy(f32[1,16,64,128]{3,2,1,0:T(8,128)} %get-tuple-element.10) | data formatting | bytes 1048576
  73.8 0.0 copy-done
  73.8 0.7 %copy.13 = f32[1,192,1,512]{3,2,1,0:T(1,128)} copy(f32[1,192,1,512]{3,2,1,0:T(1,128)S(1)} %bitcast.2) | data formatting | bytes 786432
Async XLA Ops:
  71.8 1.9 %copy-start = (f32[192,4,1,128]{3,2,1,0:T(1,128)S(1)}, f32[192,4,1,128]{3,2,1,0:T(1,128)}, u32[]{:S(2)}) copy-start(f32[192,4,1,128]{3,2,1,0:T(1,128)} %get-tuple-element.5) | copy-start | bytes 1179652

commit v2 on v1

--- a/solution.py
+++ b/solution.py
@@ -215,28 +215,28 @@
             depth = [dx[h, r : r + 8, :] for h in range(2)]
             stiff = [kx[h, r : r + 8, :] for h in range(2)]
             half_stiff = [0.5 * stiff[h] for h in range(2)]
+            for z in range(layers):
+                pressure = [ep[h, z, r : r + 8, :] for h in range(2)]
+                turned = [pltpu.roll(pressure[h], cols - 1, 1) for h in range(2)]
+                right = [
+                    jnp.where(last_lane, turned[1], turned[0]),
+                    jnp.where(last_lane, 0.0, turned[1]),
+                ]
+                for h in range(2):
+                    wet = depth[h] > z
+                    ahead = ep[h, z, r + 1 : r + 9, :]
+                    ea[h, z, r : r + 8, :] = jnp.where(
+                        wet, ea[h, z, r : r + 8, :] - (ahead - pressure[h]), 0.0
+                    )
+                    ec[h, z, r : r + 8, :] = jnp.where(
+                        wet, ec[h, z, r : r + 8, :] - (right[h] - pressure[h]), 0.0
+                    )
             pressure = [ep[h, 0, r : r + 8, :] for h in range(2)]
             wet = [depth[h] > 0 for h in range(2)]
             down = [zero, zero]
             seafloor = [zero, zero]
             for z in range(layers):
-                turned = [pltpu.roll(pressure[h], cols - 1, 1) for h in range(2)]
-                right = [
-                    jnp.where(last_lane, turned[1], turned[0]),
-                    jnp.where(last_lane, 0.0, turned[1]),
-                ]
-                along = []
-                cross = []
-                for h in range(2):
-                    ahead = ep[h, z, r + 1 : r + 9, :]
-                    value = jnp.where(wet[h], ea[h, z, r : r + 8, :] - (ahead - pressure[h]), 0.0)
-                    ea[h, z, r : r + 8, :] = value
-                    along.append(value)
-                    value = jnp.where(
-                        wet[h], ec[h, z, r : r + 8, :] - (right[h] - pressure[h]), 0.0
-                    )
-                    ec[h, z, r : r + 8, :] = value
-                    cross.append(value)
+                cross = [ec[h, z, r : r + 8, :] for h in range(2)]
                 turned = [pltpu.roll(cross[h], 1, 1) for h in range(2)]
                 left = [
                     jnp.where(first_lane, 0.0, turned[0]),
@@ -244,7 +244,7 @@
                 ]
                 for h in range(2):
                     behind = ea[h, z, r - 1 : r + 7, :]
-                    spread = (along[h] - behind) + (cross[h] - left[h])
+                    spread = (ea[h, z, r : r + 8, :] - behind) + (cross[h] - left[h])
                     if z + 1 < layers:
                         lower = ep[h, z + 1, r : r + 8, :]
                         wet_lower = depth[h] > z + 1

time: 74.6 us -> 44.9 us (0.60)
  Pallas kernels: 71.2 us -> 41.5 us
    pallas_call x1, Pallas kernels: 71.2 us -> 41.5 us  [shards(): pl.pallas_call(functools.partial(kernel, n_along, layers, rows, cols, cap...]
where the time goes in v2:
time: 44.9 us; the launch traced here: 44.8 us
  Pallas kernels  41.5 us (92%)
  local copies, waits for them, and re-layouts  2.68 us (6%)
  between operations  0.65 us (1%)
    pallas_call x1, Pallas kernels, shards(): pl.pallas_call(functools.partial(kernel, n_along, layers, rows, cols, cap...  41.5 us
    unnamed x4, local copies, waits for them, and re-layouts  2.68 us

profile of v2, /device:TPU:1, one launch (start us, length us, event | category | flops | bytes accessed | tf_op | source)
XLA Modules:
  0.0 44.8 jit_solution(1149073142115013915)
XLA Ops:
  0.6 41.5 %shard_map.86 = (f32[1,16,64,128]{3,2,1,0:T(8,128)}, f32[192,4,1,128]{3,2,1,0:T(1,128)}) custom-call(f32[1,16,64,128]{3,2,1,0:T(8,128)} %p_hbm.1, f32[1,16,64,128]{3,2,1,0:T(8,128)} %fa_hbm.1, f32[1,16,64,128]{3,2,1,0:T(8,128)} %fc_hbm.1, s32[64,128]{1,0:T(8,128)} %d_hbm.1, f32[64,128]{1,0:T(8,128)} %k_hbm.1, s32[32,128]{1,0:T(8,128)} %bitcast.3, ...), custom_call_target="tpu_custom_call" | custom-call | tf_op jit(solution)/shard_map/pallas_call | solution.py:372
  42.1 0.0 copy-start
  42.1 1.9 %copy.12 = f32[1,16,64,128]{3,2,1,0:T(8,128)} copy(f32[1,16,64,128]{3,2,1,0:T(8,128)} %get-tuple-element.10) | data formatting | bytes 1048576
  44.1 0.0 copy-done
  44.1 0.7 %copy.13 = f32[1,192,1,512]{3,2,1,0:T(1,128)} copy(f32[1,192,1,512]{3,2,1,0:T(1,128)S(1)} %bitcast.2) | data formatting | bytes 786432
Async XLA Ops:
  42.1 1.9 %copy-start = (f32[192,4,1,128]{3,2,1,0:T(1,128)S(1)}, f32[192,4,1,128]{3,2,1,0:T(1,128)}, u32[]{:S(2)}) copy-start(f32[192,4,1,128]{3,2,1,0:T(1,128)} %get-tuple-element.5) | copy-start | bytes 1179652

commit v3 on v2

--- a/solution.py
+++ b/solution.py
@@ -47,6 +47,7 @@
     panel_send,
     panel_recv,
     final_sem,
+    round_sem,
 ):
     i = lax.axis_index("along")
     j = lax.axis_index("cross")
@@ -87,16 +88,15 @@
         copy.start()
         own_copies.append(copy)
 
+    after_chip = lax.rem(i + 1, n_along)
+    before_chip = lax.rem(i + n_along - 1, n_along)
     barrier = pltpu.get_barrier_semaphore()
-
-    def greet(k, carry):
-        o = lax.rem(block + k, n_owners)
-        pl.semaphore_signal(
-            barrier, inc=1, device_id={"along": o // 2, "cross": lax.rem(o, 2)}, device_id_type=MESH
-        )
-        return carry
-
-    lax.fori_loop(1, n_owners, greet, 0)
+    pl.semaphore_signal(barrier, inc=1, device_id={"cross": other}, device_id_type=MESH)
+    for chip in (after_chip, before_chip):
+        for core in range(2):
+            pl.semaphore_signal(
+                barrier, inc=1, device_id={"along": chip, "cross": core}, device_id_type=MESH
+            )
 
     for index, (src, dst) in enumerate(fields):
         if len(dst.shape) == 4:
@@ -133,10 +133,8 @@
     held = jnp.where(mine & (rank == slot_rank), jnp.where(member[0:1, :] > 0.5, 1.0, 0.0), 0.0)
     place[...] = held.astype(jnp.bfloat16)
 
-    pl.semaphore_wait(barrier, n_owners - 1)
-
-    after_chip = lax.rem(i + 1, n_along)
-    before_chip = lax.rem(i + n_along - 1, n_along)
+    pl.semaphore_wait(barrier, 5)
+
     sends = []
     for index, (src, dst) in enumerate(fields):
         sends.append(
@@ -169,8 +167,21 @@
                 device_id_type=MESH,
             )
         )
-    for copy in sends:
+    for copy in sends[0::3] + sends[1::3] + sends[2::3]:
         copy.start()
+
+    reach = 1
+    while reach < n_along // 2:
+        for away in (reach, n_along - reach):
+            pl.semaphore_signal(
+                round_sem.at[reach.bit_length() - 1],
+                inc=1,
+                device_id={"along": lax.rem(i + away, n_along)},
+                device_id_type=MESH,
+            )
+        pl.semaphore_wait(round_sem.at[reach.bit_length() - 1], 2)
+        reach *= 2
+
     for copy in own_copies:
         copy.wait()
     for index, (src, dst) in enumerate(fields):
@@ -209,7 +220,8 @@
             device_id_type=MESH,
         )
 
-    def step(t):
+    def step(t, between=()):
+        share = -(-len(between) // tiles)
         for tile in range(tiles):
             r = PAD + 8 * tile
             depth = [dx[h, r : r + 8, :] for h in range(2)]
@@ -260,6 +272,8 @@
                         pressure[h] = lower
                         wet[h] = wet_lower
                         down[h] = up
+            for emit in between[share * tile : share * (tile + 1)]:
+                emit()
             if tile in own_tiles:
                 at = 8 * (tile - HALO // 8)
                 trace[t, pl.ds(pl.multiple_of(own_start + at, 8), 8), :] = jnp.where(
@@ -268,14 +282,20 @@
                 trace_out[t, at : at + 8, :] = jnp.where(j == 0, seafloor[1], seafloor[0])
         trace_copy(t).start()
 
-    def panel_copy(g, k):
-        o = lax.rem(block + k, n_owners)
+    order = []
+    for away in range(n_along // 2, 0, -1):
+        order += [away] if away == n_along // 2 else [away, n_along - away]
+    targets = [(lax.rem(i + away, n_along), core) for away in order for core in (j, other)]
+    targets.append((i, other))
+
+    def panel_copy(g, target):
+        chip, core = target
         return pltpu.make_async_remote_copy(
-            src_ref=outgoing.at[g, pl.ds(o * cap, cap)],
+            src_ref=outgoing.at[g, pl.ds((2 * chip + core) * cap, cap)],
             dst_ref=out_s.at[pl.ds(block * cap, cap), g],
             send_sem=panel_send.at[g],
             recv_sem=panel_recv.at[g],
-            device_id={"along": o // 2, "cross": lax.rem(o, 2)},
+            device_id={"along": chip, "cross": core},
             device_id_type=MESH,
         )
 
@@ -286,8 +306,7 @@
             final_sem.at[2 + g],
         )
 
-    def send_group(g):
-        pair = []
+    def fill_group(g):
         for s in range(2):
             trace_copy(2 * g + s).wait_recv()
         first, second = trace[2 * g], trace[2 * g + 1]
@@ -303,11 +322,8 @@
         outgoing[g, :, 0, :] = total
         own_panel_copy(g).start()
 
-        def send(k, carry):
-            panel_copy(g, k).start()
-            return carry
-
-        lax.fori_loop(1, n_owners, send, 0)
+    def group_sends(g):
+        return [functools.partial(lambda target: panel_copy(g, target).start(), t) for t in targets]
 
     own_pressure = pltpu.make_async_copy(
         ep.at[j, :, pl.ds(PAD + HALO, half), :],
@@ -323,23 +339,24 @@
         device_id_type=MESH,
     )
 
-    def advance(t, carry):
-        @pl.when(t < STEPS)
-        def _():
-            step(t)
-
-        @pl.when(t == STEPS - 1)
-        def _():
-            own_pressure.start()
-            other_pressure.start()
-
-        @pl.when((t >= 2) & (lax.rem(t, 2) == 0))
-        def _():
-            send_group(t // 2 - 1)
-
+    def first_steps(t, carry):
+        step(t)
         return carry
 
-    lax.fori_loop(0, STEPS + 1, advance, 0)
+    def advance(g, carry):
+        step(2 * g + 2)
+        fill_group(g)
+        step(2 * g + 3, group_sends(g))
+        return carry
+
+    groups = STEPS // 2
+    lax.fori_loop(0, 2, first_steps, 0)
+    lax.fori_loop(0, groups - 1, advance, 0)
+    own_pressure.start()
+    other_pressure.start()
+    fill_group(groups - 1)
+    for emit in group_sends(groups - 1):
+        emit()
 
     for copy in sends:
         copy.wait_send()
@@ -397,6 +414,7 @@
             pltpu.SemaphoreType.DMA((STEPS // 2,)),
             pltpu.SemaphoreType.DMA((STEPS // 2,)),
             pltpu.SemaphoreType.DMA((7,)),
+            pltpu.SemaphoreType.REGULAR((max(1, n_along.bit_length() - 2),)),
         ],
         compiler_params=pltpu.CompilerParams(collective_id=0, has_side_effects=True),
     )(

time: 44.9 us -> 40.1 us (0.89)
  Pallas kernels: 41.5 us -> 36.6 us
    pallas_call x1, Pallas kernels: 41.5 us -> 36.6 us  [shards(): pl.pallas_call(functools.partial(kernel, n_along, layers, rows, cols, cap...]
where the time goes in v3:
time: 40.1 us; the launch traced here: 39.9 us
  Pallas kernels  36.6 us (91%)
  local copies, waits for them, and re-layouts  2.68 us (7%)
  between operations  0.65 us (2%)
    pallas_call x1, Pallas kernels, shards(): pl.pallas_call(functools.partial(kernel, n_along, layers, rows, cols, cap...  36.6 us
    unnamed x4, local copies, waits for them, and re-layouts  2.68 us

profile of v3, /device:TPU:1, one launch (start us, length us, event | category | flops | bytes accessed | tf_op | source)
XLA Modules:
  0.0 39.9 jit_solution(15043407273433646336)
XLA Ops:
  0.6 36.6 %shard_map.86 = (f32[1,16,64,128]{3,2,1,0:T(8,128)}, f32[192,4,1,128]{3,2,1,0:T(1,128)}) custom-call(f32[1,16,64,128]{3,2,1,0:T(8,128)} %p_hbm.1, f32[1,16,64,128]{3,2,1,0:T(8,128)} %fa_hbm.1, f32[1,16,64,128]{3,2,1,0:T(8,128)} %fc_hbm.1, s32[64,128]{1,0:T(8,128)} %d_hbm.1, f32[64,128]{1,0:T(8,128)} %k_hbm.1, s32[32,128]{1,0:T(8,128)} %bitcast.3, ...), custom_call_target="tpu_custom_call" | custom-call | tf_op jit(solution)/shard_map/pallas_call | solution.py:389
  37.2 0.0 copy-start
  37.2 1.9 %copy.12 = f32[1,16,64,128]{3,2,1,0:T(8,128)} copy(f32[1,16,64,128]{3,2,1,0:T(8,128)} %get-tuple-element.10) | data formatting | bytes 1048576
  39.1 0.0 copy-done
  39.1 0.7 %copy.13 = f32[1,192,1,512]{3,2,1,0:T(1,128)} copy(f32[1,192,1,512]{3,2,1,0:T(1,128)S(1)} %bitcast.2) | data formatting | bytes 786432
Async XLA Ops:
  37.2 1.9 %copy-start = (f32[192,4,1,128]{3,2,1,0:T(1,128)S(1)}, f32[192,4,1,128]{3,2,1,0:T(1,128)}, u32[]{:S(2)}) copy-start(f32[192,4,1,128]{3,2,1,0:T(1,128)} %get-tuple-element.5) | copy-start | bytes 1179652

commit v4 on v3

--- a/solution.py
+++ b/solution.py
@@ -10,6 +10,7 @@
 STEPS = 8
 HALO = 8
 PAD = 8
+LAG = 3
 MESH = pl.DeviceIdType.MESH
 
 
@@ -48,6 +49,8 @@
     panel_recv,
     final_sem,
     round_sem,
+    landed,
+    store_sem,
 ):
     i = lax.axis_index("along")
     j = lax.axis_index("cross")
@@ -170,17 +173,21 @@
     for copy in sends[0::3] + sends[1::3] + sends[2::3]:
         copy.start()
 
-    reach = 1
-    while reach < n_along // 2:
-        for away in (reach, n_along - reach):
+    rounds = max(1, n_along.bit_length() - 2)
+
+    def tell(index):
+        for away in (1 << index, n_along - (1 << index)):
             pl.semaphore_signal(
-                round_sem.at[reach.bit_length() - 1],
+                round_sem.at[index],
                 inc=1,
                 device_id={"along": lax.rem(i + away, n_along)},
                 device_id_type=MESH,
             )
-        pl.semaphore_wait(round_sem.at[reach.bit_length() - 1], 2)
-        reach *= 2
+
+    for index in range(rounds):
+        tell(index)
+        if index + 1 < rounds:
+            pl.semaphore_wait(round_sem.at[index], 2)
 
     for copy in own_copies:
         copy.wait()
@@ -222,64 +229,99 @@
 
     def step(t, between=()):
         share = -(-len(between) // tiles)
-        for tile in range(tiles):
+
+        def rows_of(tile):
             r = PAD + 8 * tile
-            depth = [dx[h, r : r + 8, :] for h in range(2)]
-            stiff = [kx[h, r : r + 8, :] for h in range(2)]
+            return r, slice(r, r + 8)
+
+        def flows(tile):
+            r, at = rows_of(tile)
+            depth = [dx[h, at, :] for h in range(2)]
+            ready = {}
+            for tick in range(layers + LAG):
+                if tick < layers:
+                    pressure = [ep[h, tick, at, :] for h in range(2)]
+                    ready[tick] = (
+                        pressure,
+                        [pltpu.roll(pressure[h], cols - 1, 1) for h in range(2)],
+                    )
+                z = tick - LAG
+                if z >= 0:
+                    pressure, turned = ready.pop(z)
+                    right = [
+                        jnp.where(last_lane, turned[1], turned[0]),
+                        jnp.where(last_lane, 0.0, turned[1]),
+                    ]
+                    for h in range(2):
+                        wet = depth[h] > z
+                        ahead = ep[h, z, r + 1 : r + 9, :]
+                        ea[h, z, at, :] = jnp.where(
+                            wet, ea[h, z, at, :] - (ahead - pressure[h]), 0.0
+                        )
+                        ec[h, z, at, :] = jnp.where(
+                            wet, ec[h, z, at, :] - (right[h] - pressure[h]), 0.0
+                        )
+                yield
+
+        def pressures(tile):
+            r, at = rows_of(tile)
+            depth = [dx[h, at, :] for h in range(2)]
+            stiff = [kx[h, at, :] for h in range(2)]
             half_stiff = [0.5 * stiff[h] for h in range(2)]
-            for z in range(layers):
-                pressure = [ep[h, z, r : r + 8, :] for h in range(2)]
-                turned = [pltpu.roll(pressure[h], cols - 1, 1) for h in range(2)]
-                right = [
-                    jnp.where(last_lane, turned[1], turned[0]),
-                    jnp.where(last_lane, 0.0, turned[1]),
-                ]
-                for h in range(2):
-                    wet = depth[h] > z
-                    ahead = ep[h, z, r + 1 : r + 9, :]
-                    ea[h, z, r : r + 8, :] = jnp.where(
-                        wet, ea[h, z, r : r + 8, :] - (ahead - pressure[h]), 0.0
-                    )
-                    ec[h, z, r : r + 8, :] = jnp.where(
-                        wet, ec[h, z, r : r + 8, :] - (right[h] - pressure[h]), 0.0
-                    )
-            pressure = [ep[h, 0, r : r + 8, :] for h in range(2)]
+            pressure = [ep[h, 0, at, :] for h in range(2)]
             wet = [depth[h] > 0 for h in range(2)]
             down = [zero, zero]
             seafloor = [zero, zero]
-            for z in range(layers):
-                cross = [ec[h, z, r : r + 8, :] for h in range(2)]
-                turned = [pltpu.roll(cross[h], 1, 1) for h in range(2)]
-                left = [
-                    jnp.where(first_lane, 0.0, turned[0]),
-                    jnp.where(first_lane, turned[0], turned[1]),
-                ]
-                for h in range(2):
-                    behind = ea[h, z, r - 1 : r + 7, :]
-                    spread = (ea[h, z, r : r + 8, :] - behind) + (cross[h] - left[h])
-                    if z + 1 < layers:
-                        lower = ep[h, z + 1, r : r + 8, :]
-                        wet_lower = depth[h] > z + 1
-                        up = jnp.where(wet_lower, lower - pressure[h], 0.0)
-                        vertical = up - down[h]
-                    else:
-                        vertical = -down[h]
-                    value = pressure[h] - stiff[h] * spread + half_stiff[h] * vertical
-                    value = jnp.where(wet[h], value, 0.0)
-                    ep[h, z, r : r + 8, :] = value
-                    seafloor[h] = jnp.where(wet[h], value, seafloor[h])
-                    if z + 1 < layers:
-                        pressure[h] = lower
-                        wet[h] = wet_lower
-                        down[h] = up
-            for emit in between[share * tile : share * (tile + 1)]:
-                emit()
+            ready = {}
+            for tick in range(layers + LAG):
+                if tick < layers:
+                    cross = [ec[h, tick, at, :] for h in range(2)]
+                    ready[tick] = (cross, [pltpu.roll(cross[h], 1, 1) for h in range(2)])
+                z = tick - LAG
+                if z >= 0:
+                    cross, turned = ready.pop(z)
+                    left = [
+                        jnp.where(first_lane, 0.0, turned[0]),
+                        jnp.where(first_lane, turned[0], turned[1]),
+                    ]
+                    for h in range(2):
+                        spread = (ea[h, z, at, :] - ea[h, z, r - 1 : r + 7, :]) + (
+                            cross[h] - left[h]
+                        )
+                        if z + 1 < layers:
+                            lower = ep[h, z + 1, at, :]
+                            wet_lower = depth[h] > z + 1
+                            up = jnp.where(wet_lower, lower - pressure[h], 0.0)
+                            vertical = up - down[h]
+                        else:
+                            vertical = -down[h]
+                        value = pressure[h] - stiff[h] * spread + half_stiff[h] * vertical
+                        value = jnp.where(wet[h], value, 0.0)
+                        ep[h, z, at, :] = value
+                        if tile in own_tiles:
+                            seafloor[h] = jnp.where(wet[h], value, seafloor[h])
+                        if z + 1 < layers:
+                            pressure[h], wet[h], down[h] = lower, wet_lower, up
+                yield
             if tile in own_tiles:
-                at = 8 * (tile - HALO // 8)
-                trace[t, pl.ds(pl.multiple_of(own_start + at, 8), 8), :] = jnp.where(
+                to = 8 * (tile - HALO // 8)
+                trace[t, pl.ds(pl.multiple_of(own_start + to, 8), 8), :] = jnp.where(
                     j == 0, seafloor[0], seafloor[1]
                 )
-                trace_out[t, at : at + 8, :] = jnp.where(j == 0, seafloor[1], seafloor[0])
+                trace_out[t, to : to + 8, :] = jnp.where(j == 0, seafloor[1], seafloor[0])
+
+        for tile in range(tiles + 1):
+            work = []
+            if tile < tiles:
+                work.append(flows(tile))
+            if tile > 0:
+                work.append(pressures(tile - 1))
+            for _ in range(layers + LAG + 1):
+                for part in work:
+                    next(part, None)
+            if tile < tiles:
+                for emit in between[share * tile : share * (tile + 1)]:
+                    emit()
         trace_copy(t).start()
 
     order = []
@@ -292,7 +334,7 @@
         chip, core = target
         return pltpu.make_async_remote_copy(
             src_ref=outgoing.at[g, pl.ds((2 * chip + core) * cap, cap)],
-            dst_ref=out_s.at[pl.ds(block * cap, cap), g],
+            dst_ref=landed.at[g, pl.ds(block * cap, cap)],
             send_sem=panel_send.at[g],
             recv_sem=panel_recv.at[g],
             device_id={"along": chip, "cross": core},
@@ -302,7 +344,7 @@
     def own_panel_copy(g):
         return pltpu.make_async_copy(
             outgoing.at[g, pl.ds(block * cap, cap)],
-            out_s.at[pl.ds(block * cap, cap), g],
+            landed.at[g, pl.ds(block * cap, cap)],
             final_sem.at[2 + g],
         )
 
@@ -351,6 +393,7 @@
 
     groups = STEPS // 2
     lax.fori_loop(0, 2, first_steps, 0)
+    pl.semaphore_wait(round_sem.at[rounds - 1], 2)
     lax.fori_loop(0, groups - 1, advance, 0)
     own_pressure.start()
     other_pressure.start()
@@ -365,14 +408,21 @@
     own_pressure.wait()
     other_pressure.wait()
     moved = (n_owners - 1) * cap
-    for g in range(STEPS // 2):
+    stores = []
+    for g in range(groups):
         own_panel_copy(g).wait()
         pltpu.make_async_copy(
-            outgoing.at[g, pl.ds(0, moved)], out_s.at[pl.ds(0, moved), g], panel_send.at[g]
+            outgoing.at[g, pl.ds(0, moved)], landed.at[g, pl.ds(0, moved)], panel_recv.at[g]
         ).wait()
+        copy = pltpu.make_async_copy(landed.at[g], out_s.at[:, g], store_sem.at[g])
+        copy.start()
+        stores.append(copy)
+    for g in range(groups):
         pltpu.make_async_copy(
-            outgoing.at[g, pl.ds(0, moved)], out_s.at[pl.ds(0, moved), g], panel_recv.at[g]
+            outgoing.at[g, pl.ds(0, moved)], landed.at[g, pl.ds(0, moved)], panel_send.at[g]
         ).wait()
+    for copy in stores:
+        copy.wait()
 
 
 def shards(
@@ -415,16 +465,15 @@
             pltpu.SemaphoreType.DMA((STEPS // 2,)),
             pltpu.SemaphoreType.DMA((7,)),
             pltpu.SemaphoreType.REGULAR((max(1, n_along.bit_length() - 2),)),
+            pltpu.VMEM((STEPS // 2, slots, 1, cols), jnp.float32),
+            pltpu.SemaphoreType.DMA((STEPS // 2,)),
         ],
-        compiler_params=pltpu.CompilerParams(collective_id=0, has_side_effects=True),
+        compiler_params=pltpu.CompilerParams(collective_id=0, has_side_effects=True, vmem_limit_bytes=16 << 20),
     )(
-        pressure_start,
-        along_start,
-        cross_start,
-        depth_layers,
-        stiffness,
-        lists,
-        owner_map,
+        *[
+            pltpu.with_memory_space_constraint(x, pltpu.HBM)
+            for x in (pressure_start, along_start, cross_start, depth_layers, stiffness, lists, owner_map)
+        ]
     )
     return (pressure, panels.reshape(1, slots, 1, STEPS // 2 * cols))
 

time: 40.1 us -> 37.5 us (0.935)
  Pallas kernels: 36.6 us -> 35.1 us
  local copies, waits for them, and re-layouts: 2.68 us -> 1.54 us
    pallas_call x1, Pallas kernels: 36.6 us -> 35.1 us  [shards(): pl.pallas_call(functools.partial(kernel, n_along, layers, rows, cols, cap...]
    unnamed x4 -> x2, local copies, waits for them, and re-layouts: 2.68 us -> 1.54 us
where the time goes in v4:
time: 37.5 us; the launch traced here: 37.3 us
  Pallas kernels  35.1 us (94%)
  local copies, waits for them, and re-layouts  1.54 us (4%)
  between operations  0.64 us (2%)
    pallas_call x1, Pallas kernels, shards(): pl.pallas_call(functools.partial(kernel, n_along, layers, rows, cols, cap...  35.1 us
    unnamed x2, local copies, waits for them, and re-layouts  1.54 us

profile of v4, /device:TPU:1, one launch (start us, length us, event | category | flops | bytes accessed | tf_op | source)
XLA Modules:
  0.0 37.3 jit_solution(15789703645263178407)
XLA Ops:
  0.6 35.1 %shard_map.86 = (f32[1,16,64,128]{3,2,1,0:T(8,128)S(1)}, f32[192,4,1,128]{3,2,1,0:T(1,128)S(1)}) custom-call(f32[1,16,64,128]{3,2,1,0:T(8,128)} %p_hbm.1, f32[1,16,64,128]{3,2,1,0:T(8,128)} %fa_hbm.1, f32[1,16,64,128]{3,2,1,0:T(8,128)} %fc_hbm.1, s32[64,128]{1,0:T(8,128)} %d_hbm.1, f32[64,128]{1,0:T(8,128)} %k_hbm.1, s32[32,128]{1,0:T(8,128)} %bitcast.3, ...), custom_call_target="tpu_custom_call" | custom-call | tf_op jit(solution)/shard_map/pallas_call | solution.py:439
  35.7 0.8 %copy.12 = f32[1,16,64,128]{3,2,1,0:T(8,128)} copy(f32[1,16,64,128]{3,2,1,0:T(8,128)S(1)} %get-tuple-element.10) | data formatting | bytes 1048576
  36.5 0.7 %copy.13 = f32[1,192,1,512]{3,2,1,0:T(1,128)} copy(f32[1,192,1,512]{3,2,1,0:T(1,128)S(1)} %bitcast.2) | data formatting | bytes 786432

commit v5 on v4

--- a/solution.py
+++ b/solution.py
@@ -28,7 +28,7 @@
     lists_hbm,
     owners_hbm,
     out_p,
-    out_s,
+    landed,
     ep,
     ea,
     ec,
@@ -49,8 +49,6 @@
     panel_recv,
     final_sem,
     round_sem,
-    landed,
-    store_sem,
 ):
     i = lax.axis_index("along")
     j = lax.axis_index("cross")
@@ -100,6 +98,56 @@
             pl.semaphore_signal(
                 barrier, inc=1, device_id={"along": chip, "cross": core}, device_id_type=MESH
             )
+
+    pl.semaphore_wait(barrier, 5)
+
+    sends = []
+    for index, (src, dst) in enumerate(fields):
+        sends.append(
+            pltpu.make_async_remote_copy(
+                src_ref=take(src, rows - HALO, HALO),
+                dst_ref=put(dst, j, PAD, HALO),
+                send_sem=halo_send.at[index, 0],
+                recv_sem=halo_recv.at[index, 1 + j],
+                device_id={"along": after_chip, "cross": 0},
+                device_id_type=MESH,
+            )
+        )
+        sends.append(
+            pltpu.make_async_remote_copy(
+                src_ref=take(src, 0, HALO),
+                dst_ref=put(dst, j, PAD + ext, HALO),
+                send_sem=halo_send.at[index, 1],
+                recv_sem=halo_recv.at[index, 1 + j],
+                device_id={"along": before_chip, "cross": 1},
+                device_id_type=MESH,
+            )
+        )
+        sends.append(
+            pltpu.make_async_remote_copy(
+                src_ref=take(src, first_row(other), ext),
+                dst_ref=put(dst, j, first_slot(other), ext),
+                send_sem=halo_send.at[index, 2],
+                recv_sem=halo_recv.at[index, 0],
+                device_id={"cross": other},
+                device_id_type=MESH,
+            )
+        )
+    for copy in sends[0::3] + sends[1::3] + sends[2::3]:
+        copy.start()
+
+    rounds = max(1, n_along.bit_length() - 2)
+
+    def tell(index):
+        for away in (1 << index, n_along - (1 << index)):
+            pl.semaphore_signal(
+                round_sem.at[index],
+                inc=1,
+                device_id={"along": lax.rem(i + away, n_along)},
+                device_id_type=MESH,
+            )
+
+    tell(0)
 
     for index, (src, dst) in enumerate(fields):
         if len(dst.shape) == 4:
@@ -136,78 +184,6 @@
     held = jnp.where(mine & (rank == slot_rank), jnp.where(member[0:1, :] > 0.5, 1.0, 0.0), 0.0)
     place[...] = held.astype(jnp.bfloat16)
 
-    pl.semaphore_wait(barrier, 5)
-
-    sends = []
-    for index, (src, dst) in enumerate(fields):
-        sends.append(
-            pltpu.make_async_remote_copy(
-                src_ref=take(src, rows - HALO, HALO),
-                dst_ref=put(dst, j, PAD, HALO),
-                send_sem=halo_send.at[index, 0],
-                recv_sem=halo_recv.at[index, 1 + j],
-                device_id={"along": after_chip, "cross": 0},
-                device_id_type=MESH,
-            )
-        )
-        sends.append(
-            pltpu.make_async_remote_copy(
-                src_ref=take(src, 0, HALO),
-                dst_ref=put(dst, j, PAD + ext, HALO),
-                send_sem=halo_send.at[index, 1],
-                recv_sem=halo_recv.at[index, 1 + j],
-                device_id={"along": before_chip, "cross": 1},
-                device_id_type=MESH,
-            )
-        )
-        sends.append(
-            pltpu.make_async_remote_copy(
-                src_ref=take(src, first_row(other), ext),
-                dst_ref=put(dst, j, first_slot(other), ext),
-                send_sem=halo_send.at[index, 2],
-                recv_sem=halo_recv.at[index, 0],
-                device_id={"cross": other},
-                device_id_type=MESH,
-            )
-        )
-    for copy in sends[0::3] + sends[1::3] + sends[2::3]:
-        copy.start()
-
-    rounds = max(1, n_along.bit_length() - 2)
-
-    def tell(index):
-        for away in (1 << index, n_along - (1 << index)):
-            pl.semaphore_signal(
-                round_sem.at[index],
-                inc=1,
-                device_id={"along": lax.rem(i + away, n_along)},
-                device_id_type=MESH,
-            )
-
-    for index in range(rounds):
-        tell(index)
-        if index + 1 < rounds:
-            pl.semaphore_wait(round_sem.at[index], 2)
-
-    for copy in own_copies:
-        copy.wait()
-    for index, (src, dst) in enumerate(fields):
-        for source in range(3):
-            count = ext if source == 0 else HALO
-            pltpu.make_async_copy(
-                take(src, 0, count), put(dst, 0, PAD, count), halo_recv.at[index, source]
-            ).wait()
-
-    @pl.when((i == 0) & (j == 0))
-    def _():
-        ep[:, :, PAD : PAD + HALO, :] = jnp.zeros((2, layers, HALO, cols), jnp.float32)
-        dx[:, PAD : PAD + HALO, :] = jnp.zeros((2, HALO, cols), jnp.int32)
-
-    @pl.when((i == n_along - 1) & (j == 1))
-    def _():
-        ep[:, :, PAD + ext : PAD + ext + HALO, :] = jnp.zeros((2, layers, HALO, cols), jnp.float32)
-        dx[:, PAD + ext : PAD + ext + HALO, :] = jnp.zeros((2, HALO, cols), jnp.int32)
-
     lane = lax.broadcasted_iota(jnp.int32, (8, cols), 1)
     first_lane = lane == 0
     last_lane = lane == cols - 1
@@ -227,9 +203,7 @@
             device_id_type=MESH,
         )
 
-    def step(t, between=()):
-        share = -(-len(between) // tiles)
-
+    def piece(t, flow_tiles, pressure_tiles):
         def rows_of(tile):
             r = PAD + 8 * tile
             return r, slice(r, r + 8)
@@ -312,17 +286,70 @@
 
         for tile in range(tiles + 1):
             work = []
-            if tile < tiles:
+            if tile in flow_tiles:
                 work.append(flows(tile))
-            if tile > 0:
+            if tile - 1 in pressure_tiles:
                 work.append(pressures(tile - 1))
             for _ in range(layers + LAG + 1):
                 for part in work:
                     next(part, None)
-            if tile < tiles:
-                for emit in between[share * tile : share * (tile + 1)]:
-                    emit()
+            if tile - 1 == own_tiles[-1] and len(pressure_tiles) == tiles:
+                trace_copy(t).start()
+
+    def step(t):
+        piece(t, range(tiles), range(tiles))
+
+    def early(t):
+        @pl.when(j == 0)
+        def _():
+            piece(t, range(t + 1, tiles), range(t + 2, tiles))
+
+        @pl.when(j == 1)
+        def _():
+            piece(t, range(tiles - 2 - t), range(tiles - 2 - t))
+
+    def late(t):
+        @pl.when(j == 0)
+        def _():
+            piece(t, range(t + 1), range(t + 2))
+
+        @pl.when(j == 1)
+        def _():
+            piece(t, range(tiles - 2 - t, tiles), range(tiles - 2 - t, tiles))
+
         trace_copy(t).start()
+
+    def arrived(sources):
+        for index, (src, dst) in enumerate(fields):
+            for source in sources:
+                count = ext if source == 0 else HALO
+                pltpu.make_async_copy(
+                    take(src, 0, count), put(dst, 0, PAD, count), halo_recv.at[index, source]
+                ).wait()
+
+    pl.semaphore_wait(round_sem.at[0], 2)
+    tell(1)
+    for copy in own_copies:
+        copy.wait()
+    arrived((0,))
+    early(0)
+    pl.semaphore_wait(round_sem.at[1], 2)
+    tell(2)
+    early(1)
+    for index in range(3, rounds):
+        pl.semaphore_wait(round_sem.at[index - 1], 2)
+        tell(index)
+    arrived((1, 2))
+
+    @pl.when((i == 0) & (j == 0))
+    def _():
+        ep[:, :, PAD : PAD + HALO, :] = jnp.zeros((2, layers, HALO, cols), jnp.float32)
+        dx[:, PAD : PAD + HALO, :] = jnp.zeros((2, HALO, cols), jnp.int32)
+
+    @pl.when((i == n_along - 1) & (j == 1))
+    def _():
+        ep[:, :, PAD + ext : PAD + ext + HALO, :] = jnp.zeros((2, layers, HALO, cols), jnp.float32)
+        dx[:, PAD + ext : PAD + ext + HALO, :] = jnp.zeros((2, HALO, cols), jnp.int32)
 
     order = []
     for away in range(n_along // 2, 0, -1):
@@ -381,25 +408,24 @@
         device_id_type=MESH,
     )
 
-    def first_steps(t, carry):
-        step(t)
-        return carry
-
     def advance(g, carry):
         step(2 * g + 2)
         fill_group(g)
-        step(2 * g + 3, group_sends(g))
+        for emit in group_sends(g):
+            emit()
+        step(2 * g + 3)
         return carry
 
     groups = STEPS // 2
-    lax.fori_loop(0, 2, first_steps, 0)
+    late(0)
+    late(1)
     pl.semaphore_wait(round_sem.at[rounds - 1], 2)
     lax.fori_loop(0, groups - 1, advance, 0)
-    own_pressure.start()
-    other_pressure.start()
     fill_group(groups - 1)
     for emit in group_sends(groups - 1):
         emit()
+    other_pressure.start()
+    own_pressure.start()
 
     for copy in sends:
         copy.wait_send()
@@ -408,20 +434,21 @@
     own_pressure.wait()
     other_pressure.wait()
     moved = (n_owners - 1) * cap
-    stores = []
     for g in range(groups):
         own_panel_copy(g).wait()
-        pltpu.make_async_copy(
-            outgoing.at[g, pl.ds(0, moved)], landed.at[g, pl.ds(0, moved)], panel_recv.at[g]
-        ).wait()
-        copy = pltpu.make_async_copy(landed.at[g], out_s.at[:, g], store_sem.at[g])
+        for sem in (panel_recv, panel_send):
+            pltpu.make_async_copy(
+                outgoing.at[g, pl.ds(0, moved)], landed.at[g, pl.ds(0, moved)], sem.at[g]
+            ).wait()
+
+
+def store(pressure, panels, out_p, out_s, sem):
+    copies = [pltpu.make_async_copy(pressure, out_p, sem.at[panels.shape[0]])]
+    for g in range(panels.shape[0]):
+        copies.append(pltpu.make_async_copy(panels.at[g], out_s.at[:, g], sem.at[g]))
+    for copy in copies:
         copy.start()
-        stores.append(copy)
-    for g in range(groups):
-        pltpu.make_async_copy(
-            outgoing.at[g, pl.ds(0, moved)], landed.at[g, pl.ds(0, moved)], panel_send.at[g]
-        ).wait()
-    for copy in stores:
+    for copy in copies:
         copy.wait()
 
 
@@ -440,7 +467,7 @@
         functools.partial(kernel, n_along, layers, rows, cols, cap),
         out_shape=(
             jax.ShapeDtypeStruct(pressure_start.shape, jnp.float32),
-            jax.ShapeDtypeStruct((slots, STEPS // 2, 1, cols), jnp.float32),
+            jax.ShapeDtypeStruct((STEPS // 2, slots, 1, cols), jnp.float32),
         ),
         in_specs=[any_space] * 7,
         out_specs=(any_space, any_space),
@@ -465,8 +492,6 @@
             pltpu.SemaphoreType.DMA((STEPS // 2,)),
             pltpu.SemaphoreType.DMA((7,)),
             pltpu.SemaphoreType.REGULAR((max(1, n_along.bit_length() - 2),)),
-            pltpu.VMEM((STEPS // 2, slots, 1, cols), jnp.float32),
-            pltpu.SemaphoreType.DMA((STEPS // 2,)),
         ],
         compiler_params=pltpu.CompilerParams(collective_id=0, has_side_effects=True, vmem_limit_bytes=16 << 20),
     )(
@@ -475,6 +500,17 @@
             for x in (pressure_start, along_start, cross_start, depth_layers, stiffness, lists, owner_map)
         ]
     )
+    pressure, panels = pl.pallas_call(
+        store,
+        out_shape=(
+            jax.ShapeDtypeStruct(pressure.shape, jnp.float32),
+            jax.ShapeDtypeStruct((slots, STEPS // 2, 1, cols), jnp.float32),
+        ),
+        in_specs=[any_space] * 2,
+        out_specs=(any_space, any_space),
+        scratch_shapes=[pltpu.SemaphoreType.DMA((STEPS // 2 + 1,))],
+        compiler_params=pltpu.CompilerParams(vmem_limit_bytes=1 << 20),
+    )(pressure, panels)
     return (pressure, panels.reshape(1, slots, 1, STEPS // 2 * cols))
 
 

time: 37.5 us -> 35.5 us (0.947)
  local copies, waits for them, and re-layouts: 1.54 us -> 0 us
    unnamed x2 -> x0, local copies, waits for them, and re-layouts: 1.54 us -> none
    pallas_call x1, Pallas kernels: 35.1 us -> 33.8 us  [shards(): pl.pallas_call(functools.partial(kernel, n_along, layers, rows, cols, cap...]
    pallas_call x0 -> x1, Pallas kernels: none -> 0.96 us  [shards(): pl.pallas_call(store, out_shape=(jax.ShapeDtypeStruct(pressure.shape, jnp...]
where the time goes in v5:
time: 35.5 us; the launch traced here: 35.4 us
  Pallas kernels  34.8 us (98%)
  between operations  0.64 us (2%)
    pallas_call x1, Pallas kernels, shards(): pl.pallas_call(functools.partial(kernel, n_along, layers, rows, cols, cap...  33.8 us
    pallas_call x1, Pallas kernels, shards(): pl.pallas_call(store, out_shape=(jax.ShapeDtypeStruct(pressure.shape, jnp...  0.96 us

profile of v5, /device:TPU:1, one launch (start us, length us, event | category | flops | bytes accessed | tf_op | source)
XLA Modules:
  0.0 35.4 jit_solution(10433849221673885126)
XLA Ops:
  0.6 33.8 %shard_map.86 = (f32[1,16,64,128]{3,2,1,0:T(8,128)S(1)}, f32[4,192,1,128]{3,2,1,0:T(1,128)S(1)}) custom-call(f32[1,16,64,128]{3,2,1,0:T(8,128)} %p_hbm.1, f32[1,16,64,128]{3,2,1,0:T(8,128)} %fa_hbm.1, f32[1,16,64,128]{3,2,1,0:T(8,128)} %fc_hbm.1, s32[64,128]{1,0:T(8,128)} %d_hbm.1, f32[64,128]{1,0:T(8,128)} %k_hbm.1, s32[32,128]{1,0:T(8,128)} %bitcast.2, ...), custom_call_target="tpu_custom_call" | custom-call | tf_op jit(solution)/shard_map/pallas_call | solution.py:466
  34.5 1.0 %shard_map.87 = (f32[1,16,64,128]{3,2,1,0:T(8,128)}, f32[192,4,1,128]{3,2,1,0:T(1,128)}) custom-call(f32[1,16,64,128]{3,2,1,0:T(8,128)S(1)} %get-tuple-element.6.pressure, f32[4,192,1,128]{3,2,1,0:T(1,128)S(1)} %get-tuple-element.7.panels), custom_call_target="tpu_custom_call" | custom-call | tf_op jit(solution)/shard_map/pallas_call | solution.py:503

commit v6 on v5

--- a/solution.py
+++ b/solution.py
@@ -420,7 +420,13 @@
     late(0)
     late(1)
     pl.semaphore_wait(round_sem.at[rounds - 1], 2)
-    lax.fori_loop(0, groups - 1, advance, 0)
+    lax.fori_loop(0, groups - 2, advance, 0)
+    step(STEPS - 2)
+    fill_group(groups - 2)
+    for emit in group_sends(groups - 2):
+        emit()
+    piece(STEPS - 1, range(tiles - 1), own_tiles)
+    trace_copy(STEPS - 1).start()
     fill_group(groups - 1)
     for emit in group_sends(groups - 1):
         emit()

time: 35.5 us -> 35.3 us (level)
  no operation moved by 1% of the time
where the time goes in v6:
time: 35.3 us; the launch traced here: 35.2 us
  Pallas kernels  34.6 us (98%)
  between operations  0.64 us (2%)
    pallas_call x1, Pallas kernels, shards(): pl.pallas_call(functools.partial(kernel, n_along, layers, rows, cols, cap...  33.7 us
    pallas_call x1, Pallas kernels, shards(): pl.pallas_call(store, out_shape=(jax.ShapeDtypeStruct(pressure.shape, jnp...  0.96 us

profile of v6, /device:TPU:1, one launch (start us, length us, event | category | flops | bytes accessed | tf_op | source)
XLA Modules:
  0.0 35.2 jit_solution(4299055423205415620)
XLA Ops:
  0.6 33.7 %shard_map.86 = (f32[1,16,64,128]{3,2,1,0:T(8,128)S(1)}, f32[4,192,1,128]{3,2,1,0:T(1,128)S(1)}) custom-call(f32[1,16,64,128]{3,2,1,0:T(8,128)} %p_hbm.1, f32[1,16,64,128]{3,2,1,0:T(8,128)} %fa_hbm.1, f32[1,16,64,128]{3,2,1,0:T(8,128)} %fc_hbm.1, s32[64,128]{1,0:T(8,128)} %d_hbm.1, f32[64,128]{1,0:T(8,128)} %k_hbm.1, s32[32,128]{1,0:T(8,128)} %bitcast.2, ...), custom_call_target="tpu_custom_call" | custom-call | tf_op jit(solution)/shard_map/pallas_call | solution.py:472
  34.3 1.0 %shard_map.87 = (f32[1,16,64,128]{3,2,1,0:T(8,128)}, f32[192,4,1,128]{3,2,1,0:T(1,128)}) custom-call(f32[1,16,64,128]{3,2,1,0:T(8,128)S(1)} %get-tuple-element.6.pressure, f32[4,192,1,128]{3,2,1,0:T(1,128)S(1)} %get-tuple-element.7.panels), custom_call_target="tpu_custom_call" | custom-call | tf_op jit(solution)/shard_map/pallas_call | solution.py:509
